TPU v7x, 32 devices: a whole 2x2x4 slice. The times are simulated.
32 devices in a mesh: groups: 2 (over y), seq: 4 (over z), mp: 2 (over x), branch: 2 (over core).
Axes of the slice: x: 2, y: 2, z: 4, core: 2. Of those that a mesh axis runs over, the one named last changes fastest.
Arguments:
- streams: float32 [2, 8, 256, 1152], P('branch', ('groups', 'seq')), parts along dimension 1, may hold values from -6 to 6
- modulation: float32 [2, 6, 1152], P('branch'), may hold values from -3 to 3
- s_qkv: bfloat16 [2, 1152, 3, 1152], P('branch', 'seq', None, 'mp'), may hold values from -0.1875 to 0.1875
- s_out: bfloat16 [2, 1152, 1152], P('branch', 'mp', 'seq'), may hold values from -0.25 to 0.25
- w_in: bfloat16 [2, 1152, 4608], P('branch', 'seq', 'mp'), may hold values from -0.1875 to 0.1875
- w_out: bfloat16 [2, 4608, 1152], P('branch', 'mp', 'seq'), may hold values from -0.125 to 0.125
- hint_gain: float32 [13, 1152], replicated, may hold values from 0.3 to 3
- inject_layer: int32 [4], replicated, may hold values from 0 to 12
- hint_weight: bfloat16 [1152, 1152], P('seq', 'mp'), may hold values from -0.1875 to 0.1875
- t_mod: float32 [3, 1152], replicated, may hold values from -3 to 3
- t_qkv: bfloat16 [1152, 3, 1152], P('seq', None, 'mp'), may hold values from -0.1875 to 0.1875
- t_out: bfloat16 [1152, 1152], P('mp', 'seq'), may hold values from -0.25 to 0.25
Outputs:
- main_out: float32 [8, 256, 1152], P('groups', ('seq', 'branch'), 'mp'), parts along dimension 0
There are 2 independent parts, one for each index of `groups`. A program takes and returns all parts, laid end to end along the dimension named above; an argument that names none is the same for every part. Nothing has to cross between parts.
All inputs are finite; a program needn't handle non-finite values.
Results may differ from a plain program's by a relative error of at most 0.014.
Values may be sent and summed in bfloat16 or wider, within the bound.
No kernel may reach another device: no remote copies, remote signals or barrier semaphores. Data moves between devices by JAX's collectives and lax.ppermute only.
A program may use at most 64 MiB of HBM per device.

v0:
```python
import jax
import jax.numpy as jnp
from jax import lax
from jax.sharding import PartitionSpec as P

D = 1152
HEAD_DIM = 72
HINT_LAYERS = 13


def layer_norm(value, shift, scale):
    mean = jnp.mean(value, axis=-1, keepdims=True)
    centred = value - mean
    var = jnp.mean(centred * centred, axis=-1, keepdims=True)
    return centred * lax.rsqrt(var + 1e-06) * (1.0 + scale) + shift


def attend(query, keys, values):
    scores = jnp.einsum("qhd,khd->hqk", query, keys, precision=lax.Precision.HIGHEST) / jnp.sqrt(
        jnp.float32(HEAD_DIM)
    )
    weights = jnp.exp(scores)
    weights = weights / jnp.sum(weights, axis=-1, keepdims=True)
    result = jnp.einsum("hqk,khd->qhd", weights, values, precision=lax.Precision.HIGHEST)
    return result.reshape(result.shape[0], -1)


def row_product(left, piece):
    return jnp.dot(left, piece, preferred_element_type=jnp.float32)


def on_device(
    streams,
    modulation,
    s_qkv,
    s_out,
    w_in,
    w_out,
    hint_gain,
    inject_layer,
    hint_weight,
    t_mod,
    t_qkv,
    t_out,
):
    stream = streams[0, 0]
    mods = modulation[0]
    tokens = stream.shape[0]
    quarter = s_qkv.shape[3]
    offset = lax.axis_index("mp") * quarter
    local_heads = quarter // HEAD_DIM

    def share(vector):
        return lax.dynamic_slice_in_dim(vector, offset, quarter, 0)

    normed = layer_norm(stream, mods[0], mods[1]).astype(jnp.bfloat16)
    piece = lax.all_gather(s_qkv, "seq", axis=1, tiled=True)
    qkv = row_product(normed, piece[0].reshape(piece.shape[1], 3 * quarter))
    qkv = qkv.reshape(tokens, 3, local_heads, HEAD_DIM)
    attended = attend(qkv[:, 0], qkv[:, 1], qkv[:, 2]).astype(jnp.bfloat16)
    projected = jnp.dot(
        attended,
        lax.all_gather(s_out, "seq", axis=2, tiled=True)[0],
        preferred_element_type=jnp.float32,
    )
    partial_value = lax.psum_scatter(
        projected.astype(jnp.bfloat16), "mp", scatter_dimension=1, tiled=True
    ).astype(jnp.float32)
    stream_share = (
        lax.dynamic_slice_in_dim(stream, offset, quarter, 1) + share(mods[2]) * partial_value
    )
    stream = lax.all_gather(stream_share.astype(jnp.bfloat16), "mp", axis=1, tiled=True).astype(
        stream_share.dtype
    )
    normed = layer_norm(stream, mods[3], mods[4]).astype(jnp.bfloat16)
    upward = row_product(normed, lax.all_gather(w_in, "seq", axis=1, tiled=True)[0])
    hidden = jax.nn.gelu(upward, approximate=True).astype(jnp.bfloat16)
    downward = jnp.dot(
        hidden,
        lax.all_gather(w_out, "seq", axis=2, tiled=True)[0],
        preferred_element_type=jnp.float32,
    )
    mlp_part = lax.psum_scatter(
        downward.astype(jnp.bfloat16), "mp", scatter_dimension=1, tiled=True
    ).astype(jnp.float32)
    section_out = stream_share + share(mods[5]) * mlp_part
    moved = lax.all_to_all(
        lax.all_to_all(
            section_out[None, None].astype(jnp.bfloat16),
            "seq",
            split_axis=2,
            concat_axis=1,
            tiled=True,
        ),
        "branch",
        split_axis=2,
        concat_axis=0,
        tiled=True,
    ).astype(jnp.float32)
    frames = moved.shape[1]
    positions = moved.shape[2]
    rows = frames * positions
    control = moved[0]
    main_share = moved[1].reshape(rows, quarter)
    picks = (inject_layer[:, None] == jnp.arange(HINT_LAYERS, dtype=jnp.int32)[None, :]).astype(
        jnp.float32
    )
    gain = jnp.sum(picks[:, :, None] * hint_gain[None, :, :], axis=1)
    control_whole = lax.all_gather(control.astype(jnp.bfloat16), "mp", axis=2, tiled=True).astype(
        control.dtype
    )
    hint_in = (control_whole * gain[:, None, :]).astype(jnp.bfloat16).reshape(rows, D)
    hint = row_product(hint_in, lax.all_gather(hint_weight, "seq", axis=0, tiled=True))
    joined_share = main_share + hint
    joined = lax.all_gather(joined_share.astype(jnp.bfloat16), "mp", axis=1, tiled=True).astype(
        joined_share.dtype
    )
    normed_t = layer_norm(joined, t_mod[0], t_mod[1]).astype(jnp.bfloat16)
    piece = lax.all_gather(t_qkv, "seq", axis=0, tiled=True)
    tqkv = row_product(normed_t, piece.reshape(piece.shape[0], 3 * quarter))
    tqkv = tqkv.reshape(frames, positions, 3, local_heads, HEAD_DIM).transpose(1, 0, 2, 3, 4)
    attended_t = jax.vmap(attend)(tqkv[:, :, 0], tqkv[:, :, 1], tqkv[:, :, 2])
    attended_t = attended_t.transpose(1, 0, 2).reshape(rows, quarter).astype(jnp.bfloat16)
    projected_t = jnp.dot(
        attended_t,
        lax.all_gather(t_out, "seq", axis=1, tiled=True),
        preferred_element_type=jnp.float32,
    )
    temporal_part = lax.psum_scatter(
        projected_t.astype(jnp.bfloat16), "mp", scatter_dimension=1, tiled=True
    ).astype(jnp.float32)
    result = joined_share + share(t_mod[2]) * temporal_part
    return result.reshape(frames, positions, quarter)


def solution(mesh):
    in_specs = (
        P("branch", ("groups", "seq"), None, None),
        P("branch", None, None),
        P("branch", "seq", None, "mp"),
        P("branch", "mp", "seq"),
        P("branch", "seq", "mp"),
        P("branch", "mp", "seq"),
        P(),
        P(),
        P("seq", "mp"),
        P(),
        P("seq", None, "mp"),
        P("mp", "seq"),
    )
    out_specs = P("groups", ("seq", "branch"), "mp")
    return jax.shard_map(
        on_device, mesh=mesh, in_specs=in_specs, out_specs=out_specs, check_vma=False
    )
```

profile of v0, /device:TPU:0, one launch (start us, length us, event | category | flops | bytes accessed | tf_op | source)
XLA Modules:
  0.0 556.1 jit_solution(1745419225290000428)
XLA Ops:
  6.5 0.7 all-gather.9.cloned.1.call-update
  7.3 0.7 all-gather.11.cloned.1.call-update
  8.1 0.1 reduce_sum.81
  8.2 0.3 fusion.34
  8.6 87.6 %all-gather.9.cloned.1.call-done = bf16[1,1152,3,576]{3,1,2,0:T(8,128)(2,1)} async-done(((bf16[1,288,3,576]{3,1,2,0:T(8,128)(2,1)}), bf16[1,1152,3,576]{3,1,2,0:T(8,128)(2,1)}) %all-gather.9.cloned.1.call-update) | async-done | bytes 3981328 | tf_op jit(solution)/shard_map/all_gather | solution.py:57
  96.2 6.6 %copy.53 = bf16[1,1152,3,576]{1,3,2,0:T(8,128)(2,1)} copy(bf16[1,1152,3,576]{3,1,2,0:T(8,128)(2,1)} %all-gather.9.cloned.1.call-done) | data formatting | bytes 7962624 | tf_op jit(solution)/shard_map/all_gather | solution.py:57
  102.8 3.8 fusion.45
  106.6 2.1 fusion.21
  108.7 1.7 fusion.26
  110.4 21.2 %all-gather.11.cloned.1.call-done = bf16[1,576,1152]{1,2,0:T(8,128)(2,1)} async-done(((bf16[1,576,288]{1,2,0:T(8,128)(2,1)}), bf16[1,576,1152]{1,2,0:T(8,128)(2,1)}) %all-gather.11.cloned.1.call-update) | async-done | bytes 1327120 | tf_op jit(solution)/shard_map/all_gather | solution.py:63
  131.6 2.8 convolution_convert_fusion
  134.5 0.5 all-gather.13.cloned.1.call-update
  135.0 0.5 all-gather.15.cloned.1.call-update
  135.6 0.2 constant_dynamic-slice_fusion
  135.9 0.2 copy.52
  136.1 0.1 dynamic-slice_reduce_fusion.2
  136.2 12.7 %reduce-scatter.4.cloned.1.call-done = bf16[256,576]{0,1:T(8,128)(2,1)} async-done(((bf16[256,1152]{0,1:T(8,128)(2,1)}), bf16[256,576]{0,1:T(8,128)(2,1)}) %reduce-scatter.4.cloned.1.call-update) | async-done | bytes 294928 | tf_op jit(solution)/shard_map/reduce_scatter | solution.py:66
  148.9 1.1 fusion.70
  150.0 9.3 %all_gather.32 = bf16[256,1152]{0,1:T(8,128)(2,1)S(1)} all-gather(bf16[256,576]{0,1:T(8,128)(2,1)S(1)} %fusion.70), channel_id=1, replica_groups=mesh['groups'=2,'seq'=4,'mp'=2,'branch'=2] {'mp'}, dimensions={1}, use_global_device_ids=true | all-gather | bytes 884736 | tf_op jit(solution)/shard_map/all_gather | solution.py:72
  159.2 0.2 convert_reduce_fusion
  159.4 0.2 fusion.29
  159.6 89.8 %all-gather.13.cloned.1.call-done = bf16[1,1152,2304]{2,1,0:T(8,128)(2,1)} async-done(((bf16[1,288,2304]{2,1,0:T(8,128)(2,1)}), bf16[1,1152,2304]{2,1,0:T(8,128)(2,1)}) %all-gather.13.cloned.1.call-update) | async-done | bytes 5308432 | tf_op jit(solution)/shard_map/all_gather | solution.py:76
  249.5 98.9 %all-gather.15.cloned.1.call-done = bf16[1,2304,1152]{1,2,0:T(8,128)(2,1)} async-done(((bf16[1,2304,288]{1,2,0:T(8,128)(2,1)}), bf16[1,2304,1152]{1,2,0:T(8,128)(2,1)}) %all-gather.15.cloned.1.call-update) | async-done | bytes 5308432 | tf_op jit(solution)/shard_map/all_gather | solution.py:80
  348.4 8.2 %fusion.4 = bf16[256,1152]{0,1:T(8,128)(2,1)} fusion(bf16[1,2304,1152]{1,2,0:T(8,128)(2,1)} %all-gather.15.cloned.1.call-done, bf16[1,1152,2304]{2,1,0:T(8,128)(2,1)} %all-gather.13.cloned.1.call-done, bf16[256,1152]{0,1:T(8,128)(2,1)S(1)} %all_gather.32, f32[1152]{0:T(1024)S(1)} %get-tuple-element.18, f32[1152]{0:T(1024)S(1)} %get-tuple-element.21, ...), kind=kOutput, calls=%fused_computation.6 | convolution fusion | flops 2725281792 | bytes 11807744 | tf_op jit(solution)/shard_map/dot_general | solution.py:78
  356.7 0.7 all-gather.19.cloned.1.call-update
  357.4 0.7 all-gather.17.cloned.1.call-update
  358.1 0.2 all-gather.21.cloned.1.call-start
  358.3 0.5 all-gather.21.cloned.1.call-update
  358.8 0.1 dynamic-slice_reduce_fusion.1
  358.9 11.5 %reduce-scatter.6.cloned.1.call-done = bf16[256,576]{0,1:T(8,128)(2,1)} async-done(((bf16[256,1152]{0,1:T(8,128)(2,1)}), bf16[256,576]{0,1:T(8,128)(2,1)}) %reduce-scatter.6.cloned.1.call-update) | async-done | bytes 294928 | tf_op jit(solution)/shard_map/reduce_scatter | solution.py:83
  370.4 1.2 fusion.71
  371.7 0.6 copy.55
  372.3 0.5 broadcast.136
  372.8 2.7 reduce.19
  375.5 1.1 reshape.175
  376.6 4.6 all-to-all-start
  381.2 0.1 multiply_reduce_fusion
  381.4 81.1 %all-gather.19.cloned.1.call-done = bf16[1152,3,576]{2,0,1:T(8,128)(2,1)} async-done(((bf16[288,3,576]{2,0,1:T(8,128)(2,1)}), bf16[1152,3,576]{2,0,1:T(8,128)(2,1)}) %all-gather.19.cloned.1.call-update) | async-done | bytes 3981328 | tf_op jit(solution)/shard_map/all_gather | solution.py:119
  462.4 6.6 %copy.62 = bf16[1152,3,576]{0,2,1:T(8,128)(2,1)} copy(bf16[1152,3,576]{2,0,1:T(8,128)(2,1)} %all-gather.19.cloned.1.call-done) | data formatting | bytes 7962624 | tf_op jit(solution)/shard_map/all_gather | solution.py:119
  469.0 0.6 reshape.176
  469.6 0.3 copy.56
  469.9 4.0 all_to_all.21
  474.0 0.3 copy.58
  474.3 16.0 %all-gather = bf16[1,1,4,32,1152]{3,2,1,0,4:T(4,128)(2,1)S(1)} all-gather(bf16[1,1,4,32,576]{3,2,1,0,4:T(4,128)(2,1)S(1)} %copy.58), channel_id=2, replica_groups=mesh['groups'=2,'seq'=4,'mp'=2,'branch'=2] {'mp'}, dimensions={4}, use_global_device_ids=true | all-gather | bytes 442368 | tf_op jit(solution)/shard_map/all_gather | solution.py:109
  490.4 1.2 copy.59
  491.6 0.1 copy.60
  491.8 5.7 %all-gather.17.cloned.1.call-done = bf16[1152,576]{1,0:T(8,128)(2,1)} async-done(((bf16[288,576]{1,0:T(8,128)(2,1)}), bf16[1152,576]{1,0:T(8,128)(2,1)}) %all-gather.17.cloned.1.call-update) | async-done | bytes 1327120 | tf_op jit(solution)/shard_map/all_gather | solution.py:113
  497.5 2.0 fusion.83
  499.6 6.0 %all_gather.37 = bf16[128,1152]{0,1:T(8,128)(2,1)S(1)} all-gather(bf16[128,576]{0,1:T(8,128)(2,1)S(1)} %get-tuple-element.25), channel_id=1, replica_groups=mesh['groups'=2,'seq'=4,'mp'=2,'branch'=2] {'mp'}, dimensions={1}, use_global_device_ids=true | all-gather | bytes 442368 | tf_op jit(solution)/shard_map/all_gather | solution.py:115
  505.6 0.2 convert_reduce_fusion.1
  505.8 0.2 fusion.40
  506.0 0.4 fusion.43
  506.3 0.2 copy.61
  506.5 4.3 convolution_bitcast_fusion
  510.8 0.1 slice_bitcast_fusion.7
  511.0 2.5 fusion.25
  513.5 2.6 fusion.35
  516.2 0.2 convert_element_type.127
  516.4 17.1 %all-gather.21.cloned.1.call-done = bf16[576,1152]{0,1:T(8,128)(2,1)} async-done(((bf16[576,288]{0,1:T(8,128)(2,1)}), bf16[576,1152]{0,1:T(8,128)(2,1)}) %all-gather.21.cloned.1.call-update) | async-done | bytes 1327120 | tf_op jit(solution)/shard_map/all_gather | solution.py:126
  533.4 2.6 convolution_convert_fusion.1
  536.1 0.1 dynamic-slice_reduce_fusion
  536.2 11.1 %reduce-scatter.8.cloned.1.call-done = bf16[128,576]{0,1:T(8,128)(2,1)} async-done(((bf16[128,1152]{0,1:T(8,128)(2,1)}), bf16[128,576]{0,1:T(8,128)(2,1)}) %reduce-scatter.8.cloned.1.call-update) | async-done | bytes 147472 | tf_op jit(solution)/shard_map/reduce_scatter | solution.py:129
  547.3 1.0 multiply_add_fusion
  548.4 0.9 copy.68
  (40 shorter events, 0.7 us)
Async XLA Ops:
  6.5 1.5 copy-start
  6.5 89.6 %all-gather.9.cloned.1.call-start = ((), (), s32[]{:S(2)}) async-start(), calls=%async_computation.5 | async-start | bytes 5529600 | tf_op jit(solution)/shard_map/all_gather | solution.py:57
  7.3 1.2 copy-start.3
  7.3 124.3 %all-gather.11.cloned.1.call-start = ((), (), s32[]{:S(2)}) async-start(), calls=%async_computation.6 | async-start | bytes 1843200 | tf_op jit(solution)/shard_map/all_gather | solution.py:63
  8.0 140.9 %reduce-scatter.4.cloned.1.call-start = ((), (), s32[]{:S(2)}) async-start(), calls=%async_computation.7 | async-start | bytes 884736 | tf_op jit(solution)/shard_map/reduce_scatter | solution.py:66
  134.4 115.1 %all-gather.13.cloned.1.call-start = ((), (), s32[]{:S(2)}) async-start(), calls=%async_computation.8 | async-start | bytes 6635520 | tf_op jit(solution)/shard_map/all_gather | solution.py:76
  135.0 213.4 %all-gather.15.cloned.1.call-start = ((), (), s32[]{:S(2)}) async-start(), calls=%async_computation.9 | async-start | bytes 6635520 | tf_op jit(solution)/shard_map/all_gather | solution.py:80
  135.6 234.8 %reduce-scatter.6.cloned.1.call-start = ((), (), s32[]{:S(2)}) async-start(), calls=%async_computation.10 | async-start | bytes 884736 | tf_op jit(solution)/shard_map/reduce_scatter | solution.py:83
  356.6 13.9 %copy-start.1 = (bf16[256,576]{0,1:T(8,128)(2,1)S(1)}, bf16[256,576]{0,1:T(8,128)(2,1)}, u32[]{:S(2)}) copy-start(bf16[256,576]{0,1:T(8,128)(2,1)} %reduce-scatter.4.cloned.1.call-done) | copy-start | bytes 884740
  356.6 105.8 %all-gather.19.cloned.1.call-start = ((), (), s32[]{:S(2)}) async-start(), calls=%async_computation.12 | async-start | bytes 5529600 | tf_op jit(solution)/shard_map/all_gather | solution.py:119
  357.4 140.2 %all-gather.17.cloned.1.call-start = ((), (), s32[]{:S(2)}) async-start(), calls=%async_computation.11 | async-start | bytes 1843200 | tf_op jit(solution)/shard_map/all_gather | solution.py:113
  358.1 175.3 %all-gather.21.cloned.1.call-start = ((), (), s32[]{:S(2)}) async-start(), calls=%async_computation.13 | async-start | bytes 1843200 | tf_op jit(solution)/shard_map/all_gather | solution.py:126
  371.6 9.6 %copy-start.5 = (s32[4]{0:T(128)S(1)}, s32[4]{0:T(128)}, u32[]{:S(2)}) copy-start(s32[4]{0:T(128)} %param.19) | copy-start | bytes 52
  371.6 9.5 %copy-start.2 = (f32[13,1152]{1,0:T(8,128)S(1)}, f32[13,1152]{1,0:T(8,128)}, u32[]{:S(2)}) copy-start(f32[13,1152]{1,0:T(8,128)} %param.18) | copy-start | bytes 179716
  371.7 9.7 %copy-start.4 = (f32[3,1152]{1,0:T(4,128)S(1)}, f32[3,1152]{1,0:T(4,128)}, u32[]{:S(2)}) copy-start(f32[3,1152]{1,0:T(4,128)} %param.21) | copy-start | bytes 41476
  376.6 92.4 %all-to-all-start = ((bf16[4,2,18432]{2,1,0:T(2,128)(2,1)}), bf16[4,2,18432]{2,1,0:T(2,128)(2,1)S(1)}, u32[]{:S(2)}, u32[]{:S(2)}) async-start(bf16[4,2,18432]{2,1,0:T(2,128)(2,1)} %reshape.175), calls=%async_computation.2 | async-start | bytes 589824 | tf_op jit(solution)/shard_map/all_to_all | solution.py:88
  381.2 166.1 %reduce-scatter.8.cloned.1.call-start = ((), (), s32[]{:S(2)}) async-start(), calls=%async_computation.14 | async-start | bytes 442368 | tf_op jit(solution)/shard_map/reduce_scatter | solution.py:129
Sparse Core Ops, SparseCore 0:
  8.9 87.2 all-gather.8
  97.7 33.7 all-gather.10
  134.5 14.2 reduce-scatter.3
  150.3 99.1 all-gather.12
  250.9 97.4 all-gather.14
  356.7 13.6 reduce-scatter.5
  372.0 90.3 all-gather.18
  464.0 33.4 all-gather.16
  499.1 34.2 all-gather.20
  536.2 11.0 reduce-scatter.7
where the time goes:
time: 557 us; the launch traced here: 556 us
  waiting for transfers between devices  441 us (79%)
  blocking collectives  35.3 us (6%)
  matrix products  32.7 us (6%)
  local copies, waits for them, and re-layouts  20.2 us (4%)
  between operations  13.8 us (2%)
  other arithmetic  7.89 us (1%)
    all_gather x1, waiting for transfers between devices, on_device(): lax.all_gather(w_out, 'seq', axis=2, tiled=True)[0]  98.9 us
    all_gather x1, waiting for transfers between devices, on_device(): lax.all_gather(w_in, 'seq', axis=1, tiled=True)[0]  89.8 us
    all_gather x1, waiting for transfers between devices, on_device(): piece = lax.all_gather(s_qkv, 'seq', axis=1, tiled=True)  87.6 us
    all_gather x1, waiting for transfers between devices, on_device(): piece = lax.all_gather(t_qkv, 'seq', axis=0, tiled=True)  81.1 us
    all_gather x1, waiting for transfers between devices, on_device(): lax.all_gather(s_out, 'seq', axis=2, tiled=True)[0]  21.2 us
    all_gather x1, waiting for transfers between devices, on_device(): lax.all_gather(t_out, 'seq', axis=1, tiled=True)  17.1 us
    all_gather x1, blocking collectives, on_device(): lax.all_gather(control.astype(jnp.bfloat16), 'mp', axis=2, tiled=True)  16 us
    reduce_scatter x1, waiting for transfers between devices, on_device(): lax.psum_scatter(projected.astype(jnp.bfloat16), 'mp', scatter_dimension=...  12.7 us
  transfers between devices with their start and end apart: 11, of which 10 were waited for; matrix products, arithmetic and copies ran while one was open for 8% of the time, Pallas kernels for 0%

commit v1 on v0

v1 whole, which is shorter than its diff:
```python
import functools
import math

import jax
import jax.numpy as jnp
from jax import lax
from jax.experimental import pallas as pl
from jax.experimental.pallas import tpu as pltpu
from jax.sharding import PartitionSpec as P

HEAD_DIM = 72
BF16 = jnp.bfloat16
F32 = jnp.float32
NT = (((1,), (1,)), ((), ()))
VMEM_LIMIT = 48 * 1024 * 1024


def layer_norm(value, shift, scale):
    mean = jnp.mean(value, axis=-1, keepdims=True)
    centred = value - mean
    var = jnp.mean(centred * centred, axis=-1, keepdims=True)
    return centred * lax.rsqrt(var + 1e-06) * (1.0 + scale) + shift


def head_of(shape, axis):
    return lax.broadcasted_iota(jnp.int32, shape, axis) // HEAD_DIM


def spatial_kernel(lanes, h_ref, w_ref, out_ref):
    qkv = jnp.dot(h_ref[0], w_ref[...], preferred_element_type=F32)
    tokens = qkv.shape[0]
    query = qkv[:, :lanes]
    keys = qkv[:, lanes : 2 * lanes].astype(BF16)
    values = qkv[:, 2 * lanes : 3 * lanes].astype(BF16)
    heads = lanes // HEAD_DIM
    at = jnp.zeros((tokens, lanes), F32)
    owner = head_of((tokens, lanes), 1)
    for head in range(heads):
        mine = owner == head
        scores = lax.dot_general(
            jnp.where(mine, query, 0.0).astype(BF16), keys, NT, preferred_element_type=F32
        )
        weights = jnp.exp(scores / math.sqrt(HEAD_DIM))
        total = jnp.sum(weights, axis=-1, keepdims=True)
        mixed = jnp.dot(weights.astype(BF16), values, preferred_element_type=F32)
        at = jnp.where(mine, mixed / total, at)
    padded = jnp.concatenate([jnp.zeros((tokens, 3 * lanes), F32), at], axis=1).astype(BF16)
    out_ref[0] = lax.dot_general(padded, w_ref[...], NT, preferred_element_type=F32)


def spatial_attention(h, packed):
    frames, tokens, width = h.shape
    lanes = packed.shape[1] // 4
    return pl.pallas_call(
        functools.partial(spatial_kernel, lanes),
        grid=(frames,),
        in_specs=[
            pl.BlockSpec((1, tokens, width), lambda i: (i, 0, 0)),
            pl.BlockSpec(packed.shape, lambda i: (0, 0)),
        ],
        out_specs=pl.BlockSpec((1, tokens, width), lambda i: (i, 0, 0)),
        out_shape=jax.ShapeDtypeStruct((frames, tokens, width), F32),
        compiler_params=pltpu.CompilerParams(vmem_limit_bytes=VMEM_LIMIT),
        cost_estimate=pl.CostEstimate(
            flops=8 * frames * tokens * width * width, bytes_accessed=2 * width * width, transcendentals=0
        ),
    )(h, packed)


def temporal_kernel(lanes, frames, j_ref, w_ref, mod_ref, out_ref):
    ht = layer_norm(j_ref[...].astype(F32), mod_ref[0:1], mod_ref[1:2]).astype(BF16)
    rows = ht.shape[0] // frames
    qkv = jnp.dot(ht, w_ref[...], preferred_element_type=F32).reshape(frames, rows, 4 * lanes)
    query, keys = qkv[:, :, :lanes], qkv[:, :, lanes : 2 * lanes]
    values = qkv[:, :, 2 * lanes : 3 * lanes]
    pairs = (query[:, None] * keys[None]).reshape(frames * frames * rows, lanes)
    gather = (head_of((lanes, 128), 0) == lax.broadcasted_iota(jnp.int32, (lanes, 128), 1)).astype(F32)
    spread = (head_of((128, lanes), 1) == lax.broadcasted_iota(jnp.int32, (128, lanes), 0)).astype(F32)
    scores = jnp.dot(pairs, gather, precision=lax.Precision.HIGHEST, preferred_element_type=F32)
    weights = jnp.exp(scores / math.sqrt(HEAD_DIM)).reshape(frames, frames, rows, 128)
    weights = weights / jnp.sum(weights, axis=1, keepdims=True)
    wide = jnp.dot(
        weights.reshape(frames * frames * rows, 128).astype(BF16),
        spread.astype(BF16),
        preferred_element_type=F32,
    ).reshape(frames, frames, rows, lanes)
    at = jnp.sum(wide * values[None], axis=1).reshape(frames * rows, lanes)
    padded = jnp.concatenate([jnp.zeros((frames * rows, 3 * lanes), F32), at], axis=1).astype(BF16)
    out_ref[...] = lax.dot_general(padded, w_ref[...], NT, preferred_element_type=F32)


def temporal_attention(joined, packed, t_mod, frames):
    rows, width = joined.shape
    return pl.pallas_call(
        functools.partial(temporal_kernel, packed.shape[1] // 4, frames),
        out_shape=jax.ShapeDtypeStruct((rows, width), F32),
        compiler_params=pltpu.CompilerParams(vmem_limit_bytes=VMEM_LIMIT),
        cost_estimate=pl.CostEstimate(
            flops=4 * rows * width * width, bytes_accessed=2 * width * width, transcendentals=0
        ),
    )(joined, packed, t_mod)


def on_device(
    sizes,
    streams,
    modulation,
    s_qkv,
    s_out,
    w_in,
    w_out,
    hint_gain,
    inject_layer,
    hint_weight,
    t_mod,
    t_qkv,
    t_out,
):
    n_groups, n_seq, n_mp, n_branch = (sizes[a] for a in ("groups", "seq", "mp", "branch"))
    group, plane, part, core = (lax.axis_index(a) for a in ("groups", "seq", "mp", "branch"))
    x, mods = streams[0, 0], modulation[0]
    tokens, width = x.shape
    spots = tokens // (n_seq * n_branch * n_mp)
    own_tokens = tokens // n_mp

    def pick(array, index, count, axis):
        size = array.shape[axis] // count
        picked = lax.slice_in_dim(array, 0, size, axis=axis)
        for i in range(1, count):
            picked = jnp.where(index == i, lax.slice_in_dim(array, i * size, (i + 1) * size, axis=axis), picked)
        return picked

    def hop(value, by_group, by_part):
        if by_group % n_groups == 0 and by_part % n_mp == 0:
            return value
        pairs = [
            (g * n_mp + m, (g + by_group) % n_groups * n_mp + (m + by_part) % n_mp)
            for g in range(n_groups)
            for m in range(n_mp)
        ]
        return lax.ppermute(value, ("groups", "mp"), pairs)

    spread = [(g, m) for g in range(n_groups) for m in range(n_mp)]

    def gather(piece):
        return lax.all_gather(piece, "seq", axis=0, tiled=True)

    def pack(qkv, out):
        cols = pick(qkv, group, n_groups, 2)
        return jnp.concatenate([cols[:, 0], cols[:, 1], cols[:, 2], pick(out, group, n_groups, 0).T], axis=1)

    s_packed = gather(pack(s_qkv[0], s_out[0]))
    up_w = gather(pick(w_in[0], group, n_groups, 1))
    down_w = gather(pick(w_out[0], group, n_groups, 0).T)

    def both_cores(piece):
        halves = lax.all_gather(gather(piece[None]), "branch", axis=1)
        return halves.reshape(n_seq * n_branch * piece.shape[0], piece.shape[1])

    hint_half = both_cores(pick(hint_weight, core, n_branch, 0))
    t_packed = both_cores(pick(pack(t_qkv, t_out), core, n_branch, 0))
    hint_w = lax.all_gather(hint_half, "mp", axis=1, tiled=True)

    blocks = x.reshape(n_seq * n_branch, n_mp, spots, width)
    x = jnp.concatenate(
        [
            lax.dynamic_index_in_dim(blocks, (part + i) % n_mp, 1, False).reshape(own_tokens, width)
            for i in range(n_mp)
        ],
        axis=0,
    )
    h = layer_norm(x, mods[0], mods[1]).astype(BF16)
    h = jnp.stack([hop(h, -g, 0) for g in range(n_groups)])
    partial_out = spatial_attention(h, s_packed).reshape(n_groups, n_mp, own_tokens, width)

    def sum_at_owner(values):
        total = values[0, 0].astype(F32)
        for g, m in spread[1:]:
            total = total + hop(values[g, m].astype(BF16), g, m).astype(F32)
        return total

    x1 = x[:own_tokens] + mods[2] * sum_at_owner({k: partial_out[k] for k in spread})
    h2 = layer_norm(x1, mods[3], mods[4]).astype(BF16)
    rows = jnp.concatenate([hop(h2, -g, -m) for g, m in spread], axis=0)
    hidden = jax.nn.gelu(jnp.dot(rows, up_w, preferred_element_type=F32), approximate=True).astype(BF16)
    hidden = lax.optimization_barrier(hidden)
    down = lax.dot_general(hidden, down_w, NT, preferred_element_type=F32)
    down = down.reshape(len(spread), own_tokens, width)
    y = x1 + mods[5] * sum_at_owner({k: down[i] for i, k in enumerate(spread)})

    moved = lax.all_to_all(
        y.astype(BF16).reshape(1, n_seq, n_branch, spots, width), "branch", split_axis=2, concat_axis=0, tiled=True
    ).reshape(2, n_seq * spots, width)
    layer = lax.dynamic_index_in_dim(inject_layer, plane, 0, False)
    gain = lax.dynamic_index_in_dim(hint_gain, layer, 0, False)
    hint_in = (moved[0].astype(F32) * gain).astype(BF16)
    joined = moved[1].astype(F32) + jnp.dot(hint_in, hint_w, preferred_element_type=F32)

    joined = lax.all_to_all(
        joined.astype(BF16).reshape(n_seq, spots, width), "seq", split_axis=0, concat_axis=0, tiled=True
    )
    around = jnp.stack([hop(joined, -g, -m) for g, m in spread]).reshape(n_groups, n_mp, n_seq, spots, width)
    order = [(i - part + n_mp) % n_mp for i in range(n_mp)]
    around = jnp.stack([lax.dynamic_index_in_dim(around, i, 1, False) for i in order], axis=1)
    at_in = around.transpose(2, 0, 1, 3, 4)
    partial_t = temporal_attention(at_in.reshape(-1, width), t_packed, t_mod, n_seq)
    partial_t = partial_t.reshape(n_seq, n_groups, n_mp * spots, n_mp, width // n_mp)
    sends = {
        (g, m): lax.dynamic_index_in_dim(partial_t[:, g], (part + m) % n_mp, 2, False)
        for g, m in spread
    }
    result = sum_at_owner(sends)
    mine = around[0].transpose(1, 0, 2, 3).reshape(n_seq, n_mp * spots, n_mp, width // n_mp)
    mine = lax.dynamic_index_in_dim(mine, part, 2, False).astype(F32)
    gate = lax.dynamic_index_in_dim(t_mod[2].reshape(n_mp, width // n_mp), part, 0, False)
    return mine + gate * result


def solution(mesh):
    in_specs = (
        P("branch", ("groups", "seq"), None, None),
        P("branch", None, None),
        P("branch", "seq", None, "mp"),
        P("branch", "mp", "seq"),
        P("branch", "seq", "mp"),
        P("branch", "mp", "seq"),
        P(),
        P(),
        P("seq", "mp"),
        P(),
        P("seq", None, "mp"),
        P("mp", "seq"),
    )
    out_specs = P("groups", ("seq", "branch"), "mp")
    return jax.shard_map(
        functools.partial(on_device, dict(mesh.shape)),
        mesh=mesh,
        in_specs=in_specs,
        out_specs=out_specs,
        check_vma=False,
    )
```

time: 557 us -> 318 us (0.57)
  waiting for transfers between devices: 441 us -> 189 us
  matrix products: 32.7 us -> 11.5 us
  starting transfers between devices: 5.1 us -> 19.6 us
  Pallas kernels: 0 us -> 9.57 us
  blocking collectives: 35.3 us -> 41.5 us
    all_gather x7, waiting for transfers between devices: 401 us -> 163 us  [the longest x4 129 us: gather(): return lax.all_gather(piece, 'seq', axis=0, tiled=True)]
    reduce_scatter x3 -> x0, waiting for transfers between devices: 35.3 us -> none  [the longest x1 12.7 us: on_device(): lax.psum_scatter(projected.astype(jnp.bfloat16), 'mp', scatter_dimension=...]
    ppermute x0 -> x16, waiting for transfers between devices: none -> 26 us  [hop(): return lax.ppermute(value, ('groups', 'mp'), pairs)]
    dot_general x10 -> x3, matrix products: 32.7 us -> 11.5 us  [the longest x1 5.09 us: on_device(): down = lax.dot_general(hidden, down_w, NT, preferred_element_type=F32)]
    ppermute x0 -> x16, starting transfers between devices: none -> 19.4 us  [hop(): return lax.ppermute(value, ('groups', 'mp'), pairs)]
    all_gather x3 -> x0, local copies, waits for them, and re-layouts: 14.3 us -> none  [the longest x1 6.58 us: on_device(): piece = lax.all_gather(s_qkv, 'seq', axis=1, tiled=True)]
    all_to_all x1 -> x2, blocking collectives: 4 us -> 15 us  [the longest x1 11.1 us: on_device(): lax.all_to_all(joined.astype(BF16).reshape(n_seq, spots, width), 'seq', s...]
    pallas_call x0 -> x2, Pallas kernels: none -> 9.57 us  [the longest x1 5.2 us: spatial_attention(): pl.pallas_call(functools.partial(spatial_kernel, lanes), grid=(frames,),...]
  transfers between devices with their start and end apart: 11 -> 23, of which waited for: 10 -> 14; matrix products, arithmetic and copies ran while one was open for 8% -> 9% of each run, Pallas kernels for 0% -> 2%
where the time goes in v1:
time: 318 us; the launch traced here: 317 us
  waiting for transfers between devices  189 us (59%)
  blocking collectives  41.5 us (13%)
  starting transfers between devices  19.6 us (6%)
  local copies, waits for them, and re-layouts  17.5 us (6%)
  between operations  15.9 us (5%)
  other arithmetic  12.2 us (4%)
  matrix products  11.5 us (4%)
  Pallas kernels  9.57 us (3%)
    all_gather x4, waiting for transfers between devices, gather(): return lax.all_gather(piece, 'seq', axis=0, tiled=True)  129 us
    all_gather x1, waiting for transfers between devices, on_device(): hint_w = lax.all_gather(hint_half, 'mp', axis=1, tiled=True)  34.5 us
    all_gather x1, blocking collectives, gather(): return lax.all_gather(piece, 'seq', axis=0, tiled=True)  26.5 us
    ppermute x16, waiting for transfers between devices, hop(): return lax.ppermute(value, ('groups', 'mp'), pairs)  26 us
    ppermute x16, starting transfers between devices, hop(): return lax.ppermute(value, ('groups', 'mp'), pairs)  19.4 us
    all_to_all x1, blocking collectives, on_device(): lax.all_to_all(joined.astype(BF16).reshape(n_seq, spots, width), 'seq', s...  11.1 us
    unnamed x33, local copies, waits for them, and re-layouts  6.71 us
  transfers between devices with their start and end apart: 23, of which 14 were waited for; matrix products, arithmetic and copies ran while one was open for 9% of the time, Pallas kernels for 2%

profile of v1, /device:TPU:0, one launch (start us, length us, event | category | flops | bytes accessed | tf_op | source)
XLA Modules:
  0.0 316.9 jit_solution(17831435987821843385)
XLA Ops:
  6.5 1.6 slice_select_fusion.1
  8.4 1.3 concatenate.29
  9.8 26.5 %all-gather = bf16[576,576]{1,0:T(8,128)(2,1)} all-gather(bf16[144,576]{1,0:T(8,128)(2,1)S(1)} %slice_select_fusion.4), channel_id=2, replica_groups=mesh['groups'=2,'seq'=4,'mp'=2,'branch'=2] {'seq'}, dimensions={0}, use_global_device_ids=true | all-gather | bytes 829440 | tf_op jit(solution)/shard_map/all_gather | solution.py:146
  36.4 0.9 slice_select_fusion
  37.3 0.6 copy-done.9
  37.9 0.9 select_bitcast_fusion
  38.9 1.3 constant_dynamic-slice_fusion.8
  40.4 0.6 copy-done.13
  41.4 1.1 add_convert_fusion
  42.5 1.6 collective-permute-start
  44.6 0.6 concatenate.31
  45.2 0.8 slice_select_fusion.3
  46.4 7.1 %collective-permute-done = bf16[256,1152]{1,0:T(8,128)(2,1)S(1)} collective-permute-done((bf16[256,1152]{1,0:T(8,128)(2,1)}, bf16[256,1152]{1,0:T(8,128)(2,1)S(1)}, u32[]{:S(2)}, u32[]{:S(2)}) %collective-permute-start) | collective-permute-done | bytes 589856 | tf_op jit(solution)/shard_map/ppermute | solution.py:141
  53.5 1.1 pad_maximum_fusion.1.h_ref
  54.6 17.6 %all-gather.12.cloned.1.call-done.w_ref = bf16[1152,1152]{1,0:T(8,128)(2,1)} async-done(((bf16[288,1152]{1,0:T(8,128)(2,1)}), bf16[1152,1152]{1,0:T(8,128)(2,1)}) %all-gather.12.cloned.1.call-update) | async-done | bytes 2654224 | tf_op jit(solution)/shard_map/all_gather | solution.py:146
  72.2 1.3 copy-done.1
  73.4 1.7 copy-done.3
  75.2 5.2 %shard_map.118 = f32[2,256,1152]{2,1,0:T(8,128)S(1)} custom-call(bf16[2,256,1152]{2,1,0:T(8,128)(2,1)S(1)} %copy-done.1, bf16[1152,1152]{1,0:T(8,128)(2,1)S(1)} %copy-done.3), custom_call_target="tpu_custom_call" | custom-call | flops 5435817984 | bytes 2654208 | tf_op jit(solution)/shard_map/pallas_call | solution.py:54
  80.5 0.9 slice_bitcast_fusion.3
  81.5 1.5 collective-permute-start.1
  83.0 1.5 collective-permute-start.2
  84.5 0.5 collective-permute-start.3
  85.0 2.6 copy.40
  87.7 3.9 %collective-permute-done.1 = bf16[128,1152]{1,0:T(8,128)(2,1)S(1)} collective-permute-done((bf16[128,1152]{1,0:T(8,128)(2,1)}, bf16[128,1152]{1,0:T(8,128)(2,1)S(1)}, u32[]{:S(2)}, u32[]{:S(2)}) %collective-permute-start.1) | collective-permute-done | bytes 294944 | tf_op jit(solution)/shard_map/ppermute | solution.py:141
  91.6 6.5 %collective-permute-done.2 = bf16[128,1152]{1,0:T(8,128)(2,1)} collective-permute-done((bf16[128,1152]{1,0:T(8,128)(2,1)}, bf16[128,1152]{1,0:T(8,128)(2,1)}, u32[]{:S(2)}, u32[]{:S(2)}) %collective-permute-start.2) | collective-permute-done | bytes 294944 | tf_op jit(solution)/shard_map/ppermute | solution.py:141
  98.1 1.3 fusion.50
  99.7 0.7 copy-done.5
  100.5 1.4 collective-permute-start.4
  101.8 0.8 collective-permute-start.5
  102.6 1.4 collective-permute-start.6
  104.0 37.4 %all-gather.14.cloned.1.call-done = bf16[1152,1152]{1,0:T(8,128)(2,1)} async-done(((bf16[288,1152]{1,0:T(8,128)(2,1)}), bf16[1152,1152]{1,0:T(8,128)(2,1)}) %all-gather.14.cloned.1.call-update) | async-done | bytes 2654224 | tf_op jit(solution)/shard_map/all_gather | solution.py:146
  141.5 3.7 %fusion.7 = bf16[512,1152]{1,0:T(8,128)(2,1)S(1)} fusion(bf16[1152,1152]{1,0:T(8,128)(2,1)} %all-gather.14.cloned.1.call-done, bf16[128,1152]{1,0:T(8,128)(2,1)S(1)} %collective-permute-done.6, bf16[128,1152]{1,0:T(8,128)(2,1)S(1)} %collective-permute-done.5, bf16[128,1152]{1,0:T(8,128)(2,1)S(1)} %collective-permute-done.4, ...), kind=kOutput, calls=%fused_computation.9 | convolution fusion | flops 1368981504 | bytes 5013504 | tf_op jit(solution)/shard_map/dot_general | solution.py:185
  145.1 51.8 %all-gather.16.cloned.1.call-done = bf16[1152,1152]{1,0:T(8,128)(2,1)} async-done(((bf16[288,1152]{1,0:T(8,128)(2,1)}), bf16[1152,1152]{1,0:T(8,128)(2,1)}) %all-gather.16.cloned.1.call-update) | async-done | bytes 2654224 | tf_op jit(solution)/shard_map/all_gather | solution.py:146
  196.9 5.1 %fusion.54 = (bf16[512,1152]{1,0:T(8,128)(2,1)S(1)}, f32[512,1152]{1,0:T(8,128)}) fusion(bf16[512,1152]{1,0:T(8,128)(2,1)S(1)} %fusion.7, bf16[1152,1152]{1,0:T(8,128)(2,1)} %all-gather.16.cloned.1.call-done), kind=kOutput, calls=%fused_computation.109 | convolution fusion | flops 1359544320 | bytes 7372800 | tf_op jit(solution)/shard_map/dot_general | solution.py:187
  202.1 1.5 collective-permute-start.7
  203.6 1.5 collective-permute-start.8
  205.1 0.5 collective-permute-start.9
  205.7 0.6 dynamic_slice.45
  208.2 21.7 %all-gather.22.cloned.1.call-done = bf16[576,1152]{1,0:T(8,128)(2,1)} async-done(((bf16[144,1152]{1,0:T(8,128)(2,1)}), bf16[576,1152]{1,0:T(8,128)(2,1)}) %all-gather.22.cloned.1.call-update) | async-done | bytes 1327120 | tf_op jit(solution)/shard_map/all_gather | solution.py:146
  230.0 1.3 fusion.29
  231.3 4.0 %all_to_all.20 = bf16[1,4,2,16,1152]{4,3,1,0,2:T(8,128)(2,1)S(1)} all-to-all(bf16[1,4,2,16,1152]{4,3,1,0,2:T(8,128)(2,1)S(1)} %copy.39), channel_id=1, replica_groups=mesh['groups'=2,'seq'=4,'mp'=2,'branch'=2] {'branch'}, dimensions={2} | all-to-all | bytes 589824 | tf_op jit(solution)/shard_map/all_to_all | solution.py:191
  235.3 34.5 %all-gather.18.cloned.1.call-done = bf16[1152,1152]{0,1:T(8,128)(2,1)} async-done(((bf16[1152,576]{0,1:T(8,128)(2,1)}), bf16[1152,1152]{0,1:T(8,128)(2,1)}) %all-gather.18.cloned.1.call-update) | async-done | bytes 2654224 | tf_op jit(solution)/shard_map/all_gather | solution.py:162
  269.8 2.7 fusion.8
  272.5 11.1 %all_to_all.21 = bf16[4,16,1152]{2,1,0:T(8,128)(2,1)S(1)} all-to-all(bf16[4,16,1152]{2,1,0:T(8,128)(2,1)S(1)} %bitcast.135), channel_id=1, replica_groups=mesh['groups'=2,'seq'=4,'mp'=2,'branch'=2] {'seq'}, dimensions={0} | all-to-all | bytes 294912 | tf_op jit(solution)/shard_map/all_to_all | solution.py:199
  283.6 0.6 collective-permute-start.10
  284.2 1.5 collective-permute-start.11
  285.6 1.5 collective-permute-start.12
  287.2 2.1 collective-permute-done.10
  289.3 0.9 collective-permute-done.11
  290.2 1.6 collective-permute-done.12
  292.1 1.7 copy-done.4
  293.9 4.4 %shard_map.119 = f32[256,1152]{1,0:T(8,128)S(1)} custom-call(bf16[256,1152]{1,0:T(8,128)(2,1)S(1)} %bitcast.115, bf16[1152,1152]{1,0:T(8,128)(2,1)S(1)} %bitcast.116, f32[3,1152]{1,0:T(4,128)S(1)} %copy-done.2), custom_call_target="tpu_custom_call" | custom-call | flops 1358954496 | bytes 2654208 | tf_op jit(solution)/shard_map/pallas_call | solution.py:94
  298.2 0.9 reshape.266
  299.5 0.7 constant_dynamic-slice_fusion.1
  300.2 1.0 collective-permute-start.14
  301.2 2.3 collective-permute-start.15
  303.5 0.3 constant_dynamic-slice_fusion.2
  303.8 0.5 collective-permute-start.13
  304.3 0.3 constant_dynamic-slice_fusion.3
  304.6 0.3 reshape.263
  305.3 0.3 collective-permute-done.14
  305.6 1.9 collective-permute-done.15
  307.5 1.7 collective-permute-done.13
  309.2 0.8 fusion.39
  (83 shorter events, 3.7 us)
Async XLA Ops:
  6.5 201.7 %copy-start = (f32[13,1152]{1,0:T(8,128)S(1)}, f32[13,1152]{1,0:T(8,128)}, u32[]{:S(2)}) copy-start(f32[13,1152]{1,0:T(8,128)} %param.18) | copy-start | bytes 179716
  6.5 65.6 %all-gather.12.cloned.1.call-start = ((), (), s32[]{:S(2)}) async-start(), calls=%async_computation.2 | async-start | bytes 3317760 | tf_op jit(solution)/shard_map/all_gather | solution.py:146
  6.5 1.7 copy-start.10
  8.4 1.4 copy-start.12
  9.7 26.6 %copy-start.8 = (bf16[1,288,2304]{2,1,0:T(8,128)(2,1)S(1)}, bf16[1,288,2304]{2,1,0:T(8,128)(2,1)}, u32[]{:S(2)}) copy-start(bf16[1,288,2304]{2,1,0:T(8,128)(2,1)} %param.16) | copy-start | bytes 3981316
  9.7 75.3 %all-gather.20.cloned.1.call-start = ((), (), s32[]{:S(2)}) async-start(), calls=%async_computation.6 | async-start | bytes 2211840 | tf_op jit(solution)/shard_map/all_gather | solution.py:157
  36.3 105.2 %all-gather.14.cloned.1.call-start = ((), (), s32[]{:S(2)}) async-start(), calls=%async_computation.3 | async-start | bytes 3317760 | tf_op jit(solution)/shard_map/all_gather | solution.py:146
  36.3 1.6 copy-start.9
  37.3 159.7 %all-gather.16.cloned.1.call-start = ((), (), s32[]{:S(2)}) async-start(), calls=%async_computation.4 | async-start | bytes 3317760 | tf_op jit(solution)/shard_map/all_gather | solution.py:146
  38.9 191.1 %all-gather.22.cloned.1.call-start = ((), (), s32[]{:S(2)}) async-start(), calls=%async_computation.7 | async-start | bytes 1658880 | tf_op jit(solution)/shard_map/all_gather | solution.py:146
  40.3 0.7 copy-start.13
  41.4 2.7 copy-start.11
  41.4 2.9 copy-start.7
  42.5 11.0 %collective-permute-start = (bf16[256,1152]{1,0:T(8,128)(2,1)}, bf16[256,1152]{1,0:T(8,128)(2,1)S(1)}, u32[]{:S(2)}, u32[]{:S(2)}) collective-permute-start(bf16[256,1152]{1,0:T(8,128)(2,1)} %add_convert_fusion), channel_id=1, source_target_pairs={{0,16},{2,18},{16,0},{18,2},{1,17},{3,19},{17,1},{19,3},{4,20},{6,... | collective-permute-start | bytes 1769480 | tf_op jit(solution)/shard_map/ppermute | solution.py:141
  46.0 223.8 %all-gather.18.cloned.1.call-start = ((), (), s32[]{:S(2)}) async-start(), calls=%async_computation.5 | async-start | bytes 3981312 | tf_op jit(solution)/shard_map/all_gather | solution.py:162
  72.2 1.3 copy-start.1
  73.4 1.7 copy-start.3
  81.5 10.1 %collective-permute-start.1 = (bf16[128,1152]{1,0:T(8,128)(2,1)}, bf16[128,1152]{1,0:T(8,128)(2,1)S(1)}, u32[]{:S(2)}, u32[]{:S(2)}) collective-permute-start(bf16[128,1152]{1,0:T(8,128)(2,1)} %get-tuple-element.16), channel_id=1, source_target_pairs={{0,2},{2,0},{16,18},{18,16},{1,3},{3,1},{17,19},{19,17},{4,6},{6,4... | collective-permute-start | bytes 884744 | tf_op jit(solution)/shard_map/ppermute | solution.py:141
  83.0 15.1 %collective-permute-start.2 = (bf16[128,1152]{1,0:T(8,128)(2,1)}, bf16[128,1152]{1,0:T(8,128)(2,1)}, u32[]{:S(2)}, u32[]{:S(2)}) collective-permute-start(bf16[128,1152]{1,0:T(8,128)(2,1)} %get-tuple-element.18), channel_id=1, source_target_pairs={{0,16},{2,18},{16,0},{18,2},{1,17},{3,19},{17,1},{19,3},{4,20},{6,... | collective-permute-start | bytes 884744 | tf_op jit(solution)/shard_map/ppermute | solution.py:141
  84.5 13.6 %collective-permute-start.3 = (bf16[128,1152]{1,0:T(8,128)(2,1)}, bf16[128,1152]{1,0:T(8,128)(2,1)}, u32[]{:S(2)}, u32[]{:S(2)}) collective-permute-start(bf16[128,1152]{1,0:T(8,128)(2,1)} %get-tuple-element.17), channel_id=1, source_target_pairs={{0,18},{2,16},{16,2},{18,0},{1,19},{3,17},{17,3},{19,1},{4,22},{6,... | collective-permute-start | bytes 884744 | tf_op jit(solution)/shard_map/ppermute | solution.py:141
  87.6 204.5 %all-gather.24.cloned.1.call-start = ((), (), s32[]{:S(2)}) async-start(), calls=%async_computation.8 | async-start | bytes 3981312 | tf_op jit(solution)/shard_map/all_gather | solution.py:157
  99.4 0.9 copy-start.5
  100.5 40.9 %collective-permute-start.4 = (bf16[128,1152]{1,0:T(8,128)(2,1)S(1)}, bf16[128,1152]{1,0:T(8,128)(2,1)S(1)}, u32[]{:S(2)}, u32[]{:S(2)}) collective-permute-start(bf16[128,1152]{1,0:T(8,128)(2,1)S(1)} %add_convert_fusion.1), channel_id=1, source_target_pairs={{0,2},{2,0},{16,18},{18,16},{1,3},{3,1},{17,19},{19,17},{4,6},{6,4... | collective-permute-start | bytes 884744 | tf_op jit(solution)/shard_map/ppermute | solution.py:141
  101.8 39.6 %collective-permute-start.5 = (bf16[128,1152]{1,0:T(8,128)(2,1)S(1)}, bf16[128,1152]{1,0:T(8,128)(2,1)S(1)}, u32[]{:S(2)}, u32[]{:S(2)}) collective-permute-start(bf16[128,1152]{1,0:T(8,128)(2,1)S(1)} %add_convert_fusion.1), channel_id=1, source_target_pairs={{0,16},{2,18},{16,0},{18,2},{1,17},{3,19},{17,1},{19,3},{4,20},{6,... | collective-permute-start | bytes 884744 | tf_op jit(solution)/shard_map/ppermute | solution.py:141
  102.6 38.8 %collective-permute-start.6 = (bf16[128,1152]{1,0:T(8,128)(2,1)S(1)}, bf16[128,1152]{1,0:T(8,128)(2,1)S(1)}, u32[]{:S(2)}, u32[]{:S(2)}) collective-permute-start(bf16[128,1152]{1,0:T(8,128)(2,1)S(1)} %add_convert_fusion.1), channel_id=1, source_target_pairs={{0,18},{2,16},{16,2},{18,0},{1,19},{3,17},{17,3},{19,1},{4,22},{6,... | collective-permute-start | bytes 884744 | tf_op jit(solution)/shard_map/ppermute | solution.py:141
  202.0 3.6 %copy-start.14 = (s32[4]{0:T(128)S(1)}, s32[4]{0:T(128)}, u32[]{:S(2)}) copy-start(s32[4]{0:T(128)} %param.19) | copy-start | bytes 52
  202.0 28.0 %copy-start.6 = (f32[128,1152]{1,0:T(8,128)S(1)}, f32[128,1152]{1,0:T(8,128)}, u32[]{:S(2)}) copy-start(f32[128,1152]{1,0:T(8,128)} %copy-done.5) | copy-start | bytes 1769476
  202.1 27.9 %collective-permute-start.7 = (bf16[128,1152]{1,0:T(8,128)(2,1)S(1)}, bf16[128,1152]{1,0:T(8,128)(2,1)S(1)}, u32[]{:S(2)}, u32[]{:S(2)}) collective-permute-start(bf16[128,1152]{1,0:T(8,128)(2,1)S(1)} %get-tuple-element.13), channel_id=1, source_target_pairs={{0,2},{2,0},{16,18},{18,16},{1,3},{3,1},{17,19},{19,17},{4,6},{6,4... | collective-permute-start | bytes 884744 | tf_op jit(solution)/shard_map/ppermute | solution.py:141
  203.6 26.3 %collective-permute-start.8 = (bf16[128,1152]{1,0:T(8,128)(2,1)S(1)}, bf16[128,1152]{1,0:T(8,128)(2,1)S(1)}, u32[]{:S(2)}, u32[]{:S(2)}) collective-permute-start(bf16[128,1152]{1,0:T(8,128)(2,1)S(1)} %get-tuple-element.15), channel_id=1, source_target_pairs={{0,16},{2,18},{16,0},{18,2},{1,17},{3,19},{17,1},{19,3},{4,20},{6,... | collective-permute-start | bytes 884744 | tf_op jit(solution)/shard_map/ppermute | solution.py:141
  205.1 24.9 %collective-permute-start.9 = (bf16[128,1152]{1,0:T(8,128)(2,1)S(1)}, bf16[128,1152]{1,0:T(8,128)(2,1)S(1)}, u32[]{:S(2)}, u32[]{:S(2)}) collective-permute-start(bf16[128,1152]{1,0:T(8,128)(2,1)S(1)} %get-tuple-element.14), channel_id=1, source_target_pairs={{0,18},{2,16},{16,2},{18,0},{1,19},{3,17},{17,3},{19,1},{4,22},{6,... | collective-permute-start | bytes 884744 | tf_op jit(solution)/shard_map/ppermute | solution.py:141
  269.8 17.2 %copy-start.2 = (f32[3,1152]{1,0:T(4,128)S(1)}, f32[3,1152]{1,0:T(4,128)}, u32[]{:S(2)}) copy-start(f32[3,1152]{1,0:T(4,128)} %mod_ref.1) | copy-start | bytes 41476
  283.6 5.7 %collective-permute-start.10 = (bf16[4,16,1152]{2,1,0:T(8,128)(2,1)S(1)}, bf16[4,16,1152]{2,1,0:T(8,128)(2,1)S(1)}, u32[]{:S(2)}, u32[]{:S(2)}) collective-permute-start(bf16[4,16,1152]{2,1,0:T(8,128)(2,1)S(1)} %all_to_all.21), channel_id=1, source_target_pairs={{0,2},{2,0},{16,18},{18,16},{1,3},{3,1},{17,19},{19,17},{4,6},{6,4... | collective-permute-start | bytes 442376 | tf_op jit(solution)/shard_map/ppermute | solution.py:141
  284.2 6.0 %collective-permute-start.11 = (bf16[4,16,1152]{2,1,0:T(8,128)(2,1)S(1)}, bf16[4,16,1152]{2,1,0:T(8,128)(2,1)S(1)}, u32[]{:S(2)}, u32[]{:S(2)}) collective-permute-start(bf16[4,16,1152]{2,1,0:T(8,128)(2,1)S(1)} %all_to_all.21), channel_id=1, source_target_pairs={{0,16},{2,18},{16,0},{18,2},{1,17},{3,19},{17,1},{19,3},{4,20},{6,... | collective-permute-start | bytes 442376 | tf_op jit(solution)/shard_map/ppermute | solution.py:141
  285.6 6.1 %collective-permute-start.12 = (bf16[4,16,1152]{2,1,0:T(8,128)(2,1)S(1)}, bf16[4,16,1152]{2,1,0:T(8,128)(2,1)S(1)}, u32[]{:S(2)}, u32[]{:S(2)}) collective-permute-start(bf16[4,16,1152]{2,1,0:T(8,128)(2,1)S(1)} %all_to_all.21), channel_id=1, source_target_pairs={{0,18},{2,16},{16,2},{18,0},{1,19},{3,17},{17,3},{19,1},{4,22},{6,... | collective-permute-start | bytes 442376 | tf_op jit(solution)/shard_map/ppermute | solution.py:141
  292.1 1.8 copy-start.4
  300.2 5.4 %collective-permute-start.14 = (bf16[4,32,576]{2,1,0:T(8,128)(2,1)S(1)}, bf16[4,32,576]{2,1,0:T(8,128)(2,1)S(1)}, u32[]{:S(2)}, u32[]{:S(2)}) collective-permute-start(bf16[4,32,576]{2,1,0:T(8,128)(2,1)S(1)} %bitcast.139), channel_id=1, source_target_pairs={{0,16},{2,18},{16,0},{18,2},{1,17},{3,19},{17,1},{19,3},{4,20},{6,... | collective-permute-start | bytes 442376 | tf_op jit(solution)/shard_map/ppermute | solution.py:141
  301.2 6.3 %collective-permute-start.15 = (bf16[4,32,576]{2,1,0:T(8,128)(2,1)S(1)}, bf16[4,32,576]{2,1,0:T(8,128)(2,1)S(1)}, u32[]{:S(2)}, u32[]{:S(2)}) collective-permute-start(bf16[4,32,576]{2,1,0:T(8,128)(2,1)S(1)} %bitcast.140), channel_id=1, source_target_pairs={{0,18},{2,16},{16,2},{18,0},{1,19},{3,17},{17,3},{19,1},{4,22},{6,... | collective-permute-start | bytes 442376 | tf_op jit(solution)/shard_map/ppermute | solution.py:141
  303.8 5.4 %collective-permute-start.13 = (bf16[4,32,576]{2,1,0:T(8,128)(2,1)S(1)}, bf16[4,32,576]{2,1,0:T(8,128)(2,1)S(1)}, u32[]{:S(2)}, u32[]{:S(2)}) collective-permute-start(bf16[4,32,576]{2,1,0:T(8,128)(2,1)S(1)} %bitcast.141), channel_id=1, source_target_pairs={{0,2},{2,0},{16,18},{18,16},{1,3},{3,1},{17,19},{19,17},{4,6},{6,4... | collective-permute-start | bytes 442376 | tf_op jit(solution)/shard_map/ppermute | solution.py:141
Sparse Core Ops, SparseCore 0:
  9.8 62.3 all-gather.11
  73.7 9.6 all-gather.19
  84.9 56.4 all-gather.13
  142.9 54.0 all-gather.15
  198.4 31.5 all-gather.21
  231.3 38.4 all-gather.17
  271.4 11.3 all-gather.23

commit v2 on v1

--- a/solution.py
+++ b/solution.py
@@ -142,24 +142,62 @@
 
     spread = [(g, m) for g in range(n_groups) for m in range(n_mp)]
 
-    def gather(piece):
-        return lax.all_gather(piece, "seq", axis=0, tiled=True)
+    def along(value, axis, step):
+        count = sizes[axis]
+        return lax.ppermute(value, axis, [(i, (i + step) % count) for i in range(count)])
+
+    def after(value, *others):
+        return lax.optimization_barrier((value, *others))[0]
+
+    class Ring:
+        def __init__(self, piece):
+            self.piece = piece
+            self.ringed = n_seq == 4
+            if self.ringed:
+                self.first = (along(piece, "seq", 1), along(piece, "seq", -1))
+            else:
+                self.first = (lax.all_gather(piece, "seq", axis=0),)
+
+        def whole(self):
+            if not self.ringed:
+                return self.first[0].reshape(-1, self.piece.shape[1])
+            below, above = self.first
+            cut = self.piece.shape[0] // 2
+            far = jnp.concatenate([along(below[:cut], "seq", 1), along(above[cut:], "seq", -1)], axis=0)
+            full = jnp.zeros((n_seq, *self.piece.shape), self.piece.dtype)
+            for value, step in ((self.piece, 0), (below, n_seq - 1), (above, 1), (far, 2)):
+                full = lax.dynamic_update_index_in_dim(full, value, (plane + step) % n_seq, 0)
+            return full.reshape(-1, self.piece.shape[1])
+
+    def share(value, axis, index, dim):
+        if sizes[axis] != 2:
+            return lax.all_gather(value, axis, axis=dim, tiled=True)
+        other = along(value, axis, 1)
+        return jnp.where(
+            index == 0, jnp.concatenate([value, other], axis=dim), jnp.concatenate([other, value], axis=dim)
+        )
 
     def pack(qkv, out):
         cols = pick(qkv, group, n_groups, 2)
         return jnp.concatenate([cols[:, 0], cols[:, 1], cols[:, 2], pick(out, group, n_groups, 0).T], axis=1)
 
-    s_packed = gather(pack(s_qkv[0], s_out[0]))
-    up_w = gather(pick(w_in[0], group, n_groups, 1))
-    down_w = gather(pick(w_out[0], group, n_groups, 0).T)
-
-    def both_cores(piece):
-        halves = lax.all_gather(gather(piece[None]), "branch", axis=1)
-        return halves.reshape(n_seq * n_branch * piece.shape[0], piece.shape[1])
-
-    hint_half = both_cores(pick(hint_weight, core, n_branch, 0))
-    t_packed = both_cores(pick(pack(t_qkv, t_out), core, n_branch, 0))
-    hint_w = lax.all_gather(hint_half, "mp", axis=1, tiled=True)
+    def both_cores(piece, rows):
+        joined = share(piece.reshape(n_seq, 1, rows, piece.shape[1]), "branch", core, 1)
+        return joined.reshape(n_seq * n_branch * rows, piece.shape[1])
+
+    s_ring = Ring(pack(s_qkv[0], s_out[0]))
+    up_ring = Ring(pick(w_in[0], group, n_groups, 1))
+    down_ring = Ring(after(pick(w_out[0], group, n_groups, 0).T, *s_ring.first))
+    hint_piece = pick(hint_weight, core, n_branch, 0)
+    hint_ring = Ring(after(hint_piece, *up_ring.first))
+    t_piece = pick(pack(t_qkv, t_out), core, n_branch, 0)
+    t_ring = Ring(after(t_piece, *down_ring.first))
+
+    s_packed = s_ring.whole()
+    up_w = up_ring.whole()
+    down_w = down_ring.whole()
+    hint_w = both_cores(share(hint_ring.whole(), "mp", part, 1), hint_piece.shape[0])
+    t_packed = both_cores(t_ring.whole(), t_piece.shape[0])
 
     blocks = x.reshape(n_seq * n_branch, n_mp, spots, width)
     x = jnp.concatenate(

time: 318 us -> 233 us (0.73)
  waiting for transfers between devices: 189 us -> 108 us
  starting transfers between devices: 19.6 us -> 58.4 us
  blocking collectives: 41.5 us -> 3.95 us
  between operations: 15.9 us -> 2.81 us
  other arithmetic: 12.2 us -> 18.6 us
  local copies, waits for them, and re-layouts: 17.5 us -> 23.6 us
  matrix products: 11.5 us -> 6.8 us
    all_gather x7 -> x0, waiting for transfers between devices: 163 us -> none  [the longest x4 129 us: gather(): return lax.all_gather(piece, 'seq', axis=0, tiled=True)]
    ppermute x0 -> x23, waiting for transfers between devices: none -> 91.7 us  [along(): lax.ppermute(value, axis, [(i, (i + step) % count) for i in range(count)])]
    ppermute x0 -> x23, starting transfers between devices: none -> 32.5 us  [along(): lax.ppermute(value, axis, [(i, (i + step) % count) for i in range(count)])]
    all_gather x1 -> x0, blocking collectives: 26.5 us -> none  [gather(): return lax.all_gather(piece, 'seq', axis=0, tiled=True)]
    ppermute x16, waiting for transfers between devices: 26 us -> 9.89 us  [hop(): return lax.ppermute(value, ('groups', 'mp'), pairs)]
    all_to_all x1 -> x0, blocking collectives: 11.1 us -> none  [on_device(): lax.all_to_all(joined.astype(BF16).reshape(n_seq, spots, width), 'seq', s...]
    dynamic_update_slice x0 -> x14, local copies, waits for them, and re-layouts: none -> 8.09 us  [whole(): lax.dynamic_update_index_in_dim(full, value, (plane + step) % n_seq, 0)]
    all_to_all x0 -> x1, waiting for transfers between devices: none -> 6.44 us  [on_device(): lax.all_to_all(joined.astype(BF16).reshape(n_seq, spots, width), 'seq', s...]
  transfers between devices with their start and end apart: 23 -> 40, of which waited for: 14 -> 17; matrix products, arithmetic and copies ran while one was open for 9% -> 18% of each run, Pallas kernels for 2% -> 2%
where the time goes in v2:
time: 233 us; the launch traced here: 232 us
  waiting for transfers between devices  108 us (46%)
  starting transfers between devices  58.4 us (25%)
  local copies, waits for them, and re-layouts  23.6 us (10%)
  other arithmetic  18.6 us (8%)
  Pallas kernels  9.64 us (4%)
  matrix products  6.8 us (3%)
  blocking collectives  3.95 us (2%)
  between operations  2.81 us (1%)
    ppermute x23, waiting for transfers between devices, along(): lax.ppermute(value, axis, [(i, (i + step) % count) for i in range(count)])  91.7 us
    ppermute x23, starting transfers between devices, along(): lax.ppermute(value, axis, [(i, (i + step) % count) for i in range(count)])  32.5 us
    ppermute x16, starting transfers between devices, hop(): return lax.ppermute(value, ('groups', 'mp'), pairs)  22.5 us
    ppermute x16, waiting for transfers between devices, hop(): return lax.ppermute(value, ('groups', 'mp'), pairs)  9.89 us
    dynamic_update_slice x14, local copies, waits for them, and re-layouts, whole(): lax.dynamic_update_index_in_dim(full, value, (plane + step) % n_seq, 0)  8.09 us
    all_to_all x1, waiting for transfers between devices, on_device(): lax.all_to_all(joined.astype(BF16).reshape(n_seq, spots, width), 'seq', s...  6.44 us
    select_n x4, other arithmetic, pick(): jnp.where(index == i, lax.slice_in_dim(array, i * size, (i + 1) * size, a...  6.11 us
    pallas_call x1, Pallas kernels, spatial_attention(): pl.pallas_call(functools.partial(spatial_kernel, lanes), grid=(frames,),...  5.27 us
  transfers between devices with their start and end apart: 40, of which 17 were waited for; matrix products, arithmetic and copies ran while one was open for 18% of the time, Pallas kernels for 2%

profile of v2, /device:TPU:0, one launch (start us, length us, event | category | flops | bytes accessed | tf_op | source)
XLA Modules:
  0.0 231.8 jit_solution(18003546313372244584)
XLA Ops:
  0.0 1.6 slice_select_fusion.1
  1.8 1.3 concatenate.80
  3.1 3.1 %collective-permute-start.1 = (bf16[288,1152]{1,0:T(8,128)(2,1)}, bf16[288,1152]{1,0:T(8,128)(2,1)}, u32[]{:S(2)}, u32[]{:S(2)}) collective-permute-start(bf16[288,1152]{1,0:T(8,128)(2,1)} %concatenate.80), channel_id=1, source_target_pairs={{0,4},{4,8},{8,12},{12,0},{1,5},{5,9},{9,13},{13,1},{2,6},{6,10},{... | collective-permute-start | bytes 1990664 | tf_op jit(solution)/shard_map/ppermute | solution.py:147
  6.2 2.0 collective-permute-start.2
  8.2 1.7 broadcast.166.clone.1
  10.0 1.2 bitcast_dynamic-update-slice_fusion.5
  11.3 3.8 %collective-permute-start.12 = (bf16[288,1152]{1,0:T(8,128)(2,1)}, bf16[288,1152]{1,0:T(8,128)(2,1)}, u32[]{:S(2)}, u32[]{:S(2)}) collective-permute-start(bf16[288,1152]{1,0:T(8,128)(2,1)} %get-tuple-element.20), channel_id=1, source_target_pairs={{0,12},{4,0},{8,4},{12,8},{1,13},{5,1},{9,5},{13,9},{2,14},{6,2},{... | collective-permute-start | bytes 1990664 | tf_op jit(solution)/shard_map/ppermute | solution.py:147
  16.3 1.1 add_convert_fusion
  17.4 1.7 collective-permute-start
  19.4 1.3 bitcast_dynamic-update-slice_fusion.8
  21.8 1.6 slice_select_fusion.2
  24.4 2.2 concatenate.92
  26.6 1.9 slice_select_fusion.3
  28.5 1.0 slice_select_fusion.4
  32.2 1.3 fusion.12
  33.6 1.2 pad_maximum_fusion.1.h_ref
  34.8 18.1 %collective-permute-done.11 = bf16[288,1152]{1,0:T(8,128)(2,1)} collective-permute-done((bf16[288,1152]{1,0:T(8,128)(2,1)}, bf16[288,1152]{1,0:T(8,128)(2,1)}, u32[]{:S(2)}, u32[]{:S(2)}) %collective-permute-start.11) | collective-permute-done | bytes 663584 | tf_op jit(solution)/shard_map/ppermute | solution.py:147
  52.8 12.7 %collective-permute-done.12 = bf16[288,1152]{1,0:T(8,128)(2,1)} collective-permute-done((bf16[288,1152]{1,0:T(8,128)(2,1)}, bf16[288,1152]{1,0:T(8,128)(2,1)}, u32[]{:S(2)}, u32[]{:S(2)}) %collective-permute-start.12) | collective-permute-done | bytes 663584 | tf_op jit(solution)/shard_map/ppermute | solution.py:147
  65.5 1.1 collective-permute-start.22
  66.7 2.7 %collective-permute-start.23 = (bf16[144,576]{1,0:T(8,128)(2,1)S(1)}, bf16[144,576]{1,0:T(8,128)(2,1)S(1)}, u32[]{:S(2)}, u32[]{:S(2)}) collective-permute-start(bf16[144,576]{1,0:T(8,128)(2,1)S(1)} %slice_select_fusion.4), channel_id=1, source_target_pairs={{0,12},{4,0},{8,4},{12,8},{1,13},{5,1},{9,5},{13,9},{2,14},{6,2},{... | collective-permute-start | bytes 497672 | tf_op jit(solution)/shard_map/ppermute | solution.py:147
  69.4 1.0 slice.238
  71.9 1.6 collective-permute-start.3
  74.5 2.4 %collective-permute-start.14 = (bf16[144,1152]{1,0:T(8,128)(2,1)S(1)}, bf16[144,1152]{1,0:T(8,128)(2,1)S(1)}, u32[]{:S(2)}, u32[]{:S(2)}) collective-permute-start(bf16[144,1152]{1,0:T(8,128)(2,1)S(1)} %slice.246), channel_id=1, source_target_pairs={{0,12},{4,0},{8,4},{12,8},{1,13},{5,1},{9,5},{13,9},{2,14},{6,2},{... | collective-permute-start | bytes 995336 | tf_op jit(solution)/shard_map/ppermute | solution.py:147
  77.2 1.0 slice.245
  78.2 1.2 bitcast_dynamic-update-slice_fusion.7
  79.4 2.0 bitcast_dynamic-update-slice_fusion.4
  81.4 1.2 bitcast_dynamic-update-slice_fusion.6
  82.5 2.0 bitcast_dynamic-update-slice_fusion.3
  84.8 3.9 %collective-permute-start.25 = (bf16[72,576]{1,0:T(8,128)(2,1)S(1)}, bf16[72,576]{1,0:T(8,128)(2,1)S(1)}, u32[]{:S(2)}, u32[]{:S(2)}) collective-permute-start(bf16[72,576]{1,0:T(8,128)(2,1)S(1)} %slice.256), channel_id=1, source_target_pairs={{0,12},{4,0},{8,4},{12,8},{1,13},{5,1},{9,5},{13,9},{2,14},{6,2},{... | collective-permute-start | bytes 248840 | tf_op jit(solution)/shard_map/ppermute | solution.py:147
  88.8 4.3 %collective-permute-done.3 = bf16[144,1152]{1,0:T(8,128)(2,1)S(1)} collective-permute-done((bf16[144,1152]{1,0:T(8,128)(2,1)S(1)}, bf16[144,1152]{1,0:T(8,128)(2,1)S(1)}, u32[]{:S(2)}, u32[]{:S(2)}) %collective-permute-start.3) | collective-permute-done | bytes 331808 | tf_op jit(solution)/shard_map/ppermute | solution.py:147
  93.1 5.3 %shard_map.118 = f32[2,256,1152]{2,1,0:T(8,128)S(1)} custom-call(bf16[2,256,1152]{2,1,0:T(8,128)(2,1)S(1)} %pad_maximum_fusion.1.h_ref, bf16[1152,1152]{1,0:T(8,128)(2,1)S(1)} %bitcast.170), custom_call_target="tpu_custom_call" | custom-call | flops 5435817984 | bytes 2654208 | tf_op jit(solution)/shard_map/pallas_call | solution.py:54
  98.7 2.5 %collective-permute-start.7 = (bf16[128,1152]{1,0:T(8,128)(2,1)S(1)}, bf16[128,1152]{1,0:T(8,128)(2,1)S(1)}, u32[]{:S(2)}, u32[]{:S(2)}) collective-permute-start(bf16[128,1152]{1,0:T(8,128)(2,1)S(1)} %get-tuple-element.25), channel_id=1, source_target_pairs={{0,18},{2,16},{16,2},{18,0},{1,19},{3,17},{17,3},{19,1},{4,22},{6,... | collective-permute-start | bytes 884744 | tf_op jit(solution)/shard_map/ppermute | solution.py:141
  101.2 7.1 %collective-permute-done.25 = bf16[72,576]{1,0:T(8,128)(2,1)S(1)} collective-permute-done((bf16[72,576]{1,0:T(8,128)(2,1)S(1)}, bf16[72,576]{1,0:T(8,128)(2,1)S(1)}, u32[]{:S(2)}, u32[]{:S(2)}) %collective-permute-start.25) | collective-permute-done | bytes 82976 | tf_op jit(solution)/shard_map/ppermute | solution.py:147
  108.3 1.5 collective-permute-start.6
  109.8 1.5 collective-permute-start.5
  111.4 3.8 %collective-permute-start.16 = (bf16[288,1152]{1,0:T(8,128)(2,1)S(1)}, bf16[288,1152]{1,0:T(8,128)(2,1)S(1)}, u32[]{:S(2)}, u32[]{:S(2)}) collective-permute-start(bf16[288,1152]{1,0:T(8,128)(2,1)S(1)} %copy-done.4), channel_id=1, source_target_pairs={{0,12},{4,0},{8,4},{12,8},{1,13},{5,1},{9,5},{13,9},{2,14},{6,2},{... | collective-permute-start | bytes 1990664 | tf_op jit(solution)/shard_map/ppermute | solution.py:147
  116.7 1.3 collective-permute-done.5
  118.8 3.5 %collective-permute-start.10 = (bf16[128,1152]{1,0:T(8,128)(2,1)S(1)}, bf16[128,1152]{1,0:T(8,128)(2,1)S(1)}, u32[]{:S(2)}, u32[]{:S(2)}) collective-permute-start(bf16[128,1152]{1,0:T(8,128)(2,1)S(1)} %add_convert_fusion.1), channel_id=1, source_target_pairs={{0,18},{2,16},{16,2},{18,0},{1,19},{3,17},{17,3},{19,1},{4,22},{6,... | collective-permute-start | bytes 884744 | tf_op jit(solution)/shard_map/ppermute | solution.py:141
  122.8 8.2 %collective-permute-done.15 = bf16[288,1152]{1,0:T(8,128)(2,1)S(1)} collective-permute-done((bf16[288,1152]{1,0:T(8,128)(2,1)S(1)}, bf16[288,1152]{1,0:T(8,128)(2,1)S(1)}, u32[]{:S(2)}, u32[]{:S(2)}) %collective-permute-start.15) | collective-permute-done | bytes 663584 | tf_op jit(solution)/shard_map/ppermute | solution.py:147
  131.5 9.4 %collective-permute-done.16 = bf16[288,1152]{1,0:T(8,128)(2,1)S(1)} collective-permute-done((bf16[288,1152]{1,0:T(8,128)(2,1)S(1)}, bf16[288,1152]{1,0:T(8,128)(2,1)S(1)}, u32[]{:S(2)}, u32[]{:S(2)}) %collective-permute-start.16) | collective-permute-done | bytes 663584 | tf_op jit(solution)/shard_map/ppermute | solution.py:147
  140.9 1.6 collective-permute-start.31
  142.9 2.3 collective-permute-start.32
  146.5 1.7 collective-permute-start.17
  148.2 3.7 %fusion.7 = bf16[512,1152]{1,0:T(8,128)(2,1)S(1)} fusion(bf16[1152,1152]{1,0:T(8,128)(2,1)} %bitcast.27, bf16[128,1152]{1,0:T(8,128)(2,1)S(1)} %collective-permute-done.10, bf16[128,1152]{1,0:T(8,128)(2,1)S(1)} %collective-permute-done.9, bf16[128,1152]{1,0:T(8,128)(2,1)S(1)} %collective-permute-done.8, bf16[128,1152]{1,0:T(8,128)(2,1)S(1)} %add_convert_fusion.1), kind=kOutput, calls=%fused_computation.11 | convolution fusion | flops 1368981504 | bytes 5013504 | tf_op jit(solution)/shard_map/dot_general | solution.py:223
  151.9 15.7 %collective-permute-done.18 = bf16[144,1152]{1,0:T(8,128)(2,1)S(1)} collective-permute-done((bf16[144,1152]{1,0:T(8,128)(2,1)S(1)}, bf16[144,1152]{1,0:T(8,128)(2,1)S(1)}, u32[]{:S(2)}, u32[]{:S(2)}) %collective-permute-start.18) | collective-permute-done | bytes 331808 | tf_op jit(solution)/shard_map/ppermute | solution.py:147
  167.6 4.8 %collective-permute-done.17 = bf16[144,1152]{1,0:T(8,128)(2,1)S(1)} collective-permute-done((bf16[144,1152]{1,0:T(8,128)(2,1)S(1)}, bf16[144,1152]{1,0:T(8,128)(2,1)S(1)}, u32[]{:S(2)}, u32[]{:S(2)}) %collective-permute-start.17) | collective-permute-done | bytes 331808 | tf_op jit(solution)/shard_map/ppermute | solution.py:147
  172.4 1.9 fusion.56
  174.4 1.6 collective-permute-start.21
  176.5 1.5 collective-permute-start.19
  178.1 5.3 %collective-permute-done.34 = bf16[72,1152]{1,0:T(8,128)(2,1)S(1)} collective-permute-done((bf16[72,1152]{1,0:T(8,128)(2,1)S(1)}, bf16[72,1152]{1,0:T(8,128)(2,1)S(1)}, u32[]{:S(2)}, u32[]{:S(2)}) %collective-permute-start.34) | collective-permute-done | bytes 165920 | tf_op jit(solution)/shard_map/ppermute | solution.py:147
  184.2 6.3 %collective-permute-done.33 = bf16[72,1152]{1,0:T(8,128)(2,1)S(1)} collective-permute-done((bf16[72,1152]{1,0:T(8,128)(2,1)S(1)}, bf16[72,1152]{1,0:T(8,128)(2,1)S(1)}, u32[]{:S(2)}, u32[]{:S(2)}) %collective-permute-start.33) | collective-permute-done | bytes 165920 | tf_op jit(solution)/shard_map/ppermute | solution.py:147
  190.9 4.0 %all_to_all.20 = bf16[1,4,2,16,1152]{4,3,1,0,2:T(8,128)(2,1)S(1)} all-to-all(bf16[1,4,2,16,1152]{4,3,1,0,2:T(8,128)(2,1)S(1)} %copy.31), channel_id=1, replica_groups=mesh['groups'=2,'seq'=4,'mp'=2,'branch'=2] {'branch'}, dimensions={2} | all-to-all | bytes 589824 | tf_op jit(solution)/shard_map/all_to_all | solution.py:229
  195.4 1.3 fusion.8
  196.7 3.3 %all-to-all-start.1 = ((bf16[4,16,1152]{2,1,0:T(8,128)(2,1)}), bf16[4,16,1152]{2,1,0:T(8,128)(2,1)S(1)}, u32[]{:S(2)}, u32[]{:S(2)}) async-start(bf16[4,16,1152]{2,1,0:T(8,128)(2,1)} %bitcast.50), calls=%async_computation.1 | async-start | bytes 294912 | tf_op jit(solution)/shard_map/all_to_all | solution.py:237
  200.2 6.4 %all-to-all-done.1 = bf16[4,16,1152]{2,1,0:T(8,128)(2,1)S(1)} async-done(((bf16[4,16,1152]{2,1,0:T(8,128)(2,1)}), bf16[4,16,1152]{2,1,0:T(8,128)(2,1)S(1)}, u32[]{:S(2)}, u32[]{:S(2)}) %all-to-all-start.1) | async-done | bytes 147488 | tf_op jit(solution)/shard_map/all_to_all | solution.py:237
  206.7 1.5 collective-permute-start.30
  208.7 1.5 collective-permute-start.28
  210.6 2.8 %collective-permute-done.30 = bf16[4,16,1152]{2,1,0:T(8,128)(2,1)S(1)} collective-permute-done((bf16[4,16,1152]{2,1,0:T(8,128)(2,1)S(1)}, bf16[4,16,1152]{2,1,0:T(8,128)(2,1)S(1)}, u32[]{:S(2)}, u32[]{:S(2)}) %collective-permute-start.30) | collective-permute-done | bytes 147488 | tf_op jit(solution)/shard_map/ppermute | solution.py:141
  213.4 1.5 collective-permute-done.29
  215.3 4.4 %shard_map.119 = f32[256,1152]{1,0:T(8,128)S(1)} custom-call(bf16[256,1152]{1,0:T(8,128)(2,1)S(1)} %bitcast.171, bf16[1152,1152]{1,0:T(8,128)(2,1)S(1)} %bitcast.169, f32[3,1152]{1,0:T(4,128)S(1)} %copy-done.2), custom_call_target="tpu_custom_call" | custom-call | flops 1358954496 | bytes 2654208 | tf_op jit(solution)/shard_map/pallas_call | solution.py:94
  221.7 1.5 collective-permute-start.38
  224.2 1.5 collective-permute-start.36
  226.7 2.8 %collective-permute-done.38 = bf16[4,32,576]{2,1,0:T(8,128)(2,1)S(1)} collective-permute-done((bf16[4,32,576]{2,1,0:T(8,128)(2,1)S(1)}, bf16[4,32,576]{2,1,0:T(8,128)(2,1)S(1)}, u32[]{:S(2)}, u32[]{:S(2)}) %collective-permute-start.38) | collective-permute-done | bytes 147488 | tf_op jit(solution)/shard_map/ppermute | solution.py:141
  229.5 1.5 collective-permute-done.37
  (157 shorter events, 22.0 us)
Async XLA Ops:
  0.0 32.2 %copy-start = (f32[13,1152]{1,0:T(8,128)S(1)}, f32[13,1152]{1,0:T(8,128)}, u32[]{:S(2)}) copy-start(f32[13,1152]{1,0:T(8,128)} %param.18) | copy-start | bytes 179716
  0.0 1.7 copy-start.9
  3.1 67.8 %collective-permute-start.1 = (bf16[288,1152]{1,0:T(8,128)(2,1)}, bf16[288,1152]{1,0:T(8,128)(2,1)}, u32[]{:S(2)}, u32[]{:S(2)}) collective-permute-start(bf16[288,1152]{1,0:T(8,128)(2,1)} %concatenate.80), channel_id=1, source_target_pairs={{0,4},{4,8},{8,12},{12,0},{1,5},{5,9},{9,13},{13,1},{2,6},{6,10},{... | collective-permute-start | bytes 1990664 | tf_op jit(solution)/shard_map/ppermute | solution.py:147
  6.2 63.2 %collective-permute-start.2 = (bf16[288,1152]{1,0:T(8,128)(2,1)}, bf16[288,1152]{1,0:T(8,128)(2,1)}, u32[]{:S(2)}, u32[]{:S(2)}) collective-permute-start(bf16[288,1152]{1,0:T(8,128)(2,1)} %concatenate.80), channel_id=1, source_target_pairs={{0,12},{4,0},{8,4},{12,8},{1,13},{5,1},{9,5},{13,9},{2,14},{6,2},{... | collective-permute-start | bytes 1990664 | tf_op jit(solution)/shard_map/ppermute | solution.py:147
  8.2 1.8 copy-start.5
  10.0 5.1 %copy-start.15 = (f32[1,6,1152]{2,0,1:T(1,128)S(1)}, f32[1,6,1152]{2,0,1:T(1,128)}, u32[]{:S(2)}) copy-start(f32[1,6,1152]{2,0,1:T(1,128)} %param.13) | copy-start | bytes 82948
  10.0 5.7 %copy-start.8 = (f32[1,1,256,1152]{3,2,1,0:T(8,128)S(1)}, f32[1,1,256,1152]{3,2,1,0:T(8,128)}, u32[]{:S(2)}) copy-start(f32[1,1,256,1152]{3,2,1,0:T(8,128)} %param.12) | copy-start | bytes 3538948
  11.3 41.6 %collective-permute-start.11 = (bf16[288,1152]{1,0:T(8,128)(2,1)}, bf16[288,1152]{1,0:T(8,128)(2,1)}, u32[]{:S(2)}, u32[]{:S(2)}) collective-permute-start(bf16[288,1152]{1,0:T(8,128)(2,1)} %get-tuple-element.20), channel_id=1, source_target_pairs={{0,4},{4,8},{8,12},{12,0},{1,5},{5,9},{9,13},{13,1},{2,6},{6,10},{... | collective-permute-start | bytes 1990664 | tf_op jit(solution)/shard_map/ppermute | solution.py:147
  11.3 54.3 %collective-permute-start.12 = (bf16[288,1152]{1,0:T(8,128)(2,1)}, bf16[288,1152]{1,0:T(8,128)(2,1)}, u32[]{:S(2)}, u32[]{:S(2)}) collective-permute-start(bf16[288,1152]{1,0:T(8,128)(2,1)} %get-tuple-element.20), channel_id=1, source_target_pairs={{0,12},{4,0},{8,4},{12,8},{1,13},{5,1},{9,5},{13,9},{2,14},{6,2},{... | collective-permute-start | bytes 1990664 | tf_op jit(solution)/shard_map/ppermute | solution.py:147
  15.8 1.6 copy-start.3
  16.0 1.4 copy-start.16
  16.3 2.9 %copy-start.18 = (f32[256]{0:T(256)}, f32[256]{0:T(256)S(1)}, u32[]{:S(2)}) copy-start(f32[256]{0:T(256)S(1)} %add_rsqrt_fusion) | copy-start | bytes 3076
  17.4 16.2 %collective-permute-start = (bf16[256,1152]{1,0:T(8,128)(2,1)}, bf16[256,1152]{1,0:T(8,128)(2,1)}, u32[]{:S(2)}, u32[]{:S(2)}) collective-permute-start(bf16[256,1152]{1,0:T(8,128)(2,1)} %add_convert_fusion), channel_id=1, source_target_pairs={{0,16},{2,18},{16,0},{18,2},{1,17},{3,19},{17,1},{19,3},{4,20},{6,... | collective-permute-start | bytes 1769480 | tf_op jit(solution)/shard_map/ppermute | solution.py:141
  19.4 1.5 copy-start.7
  21.8 2.5 %copy-start.10 = (bf16[576,288]{0,1:T(8,128)(2,1)S(1)}, bf16[576,288]{0,1:T(8,128)(2,1)}, u32[]{:S(2)}) copy-start(bf16[576,288]{0,1:T(8,128)(2,1)} %param.23) | copy-start | bytes 995332
  26.6 3.0 %copy-start.20 = (s32[4]{0:T(128)S(1)}, s32[4]{0:T(128)}, u32[]{:S(2)}) copy-start(s32[4]{0:T(128)} %param.19) | copy-start | bytes 52
  26.6 5.6 %copy-start.17 = (f32[256]{0:T(256)S(1)}, f32[256]{0:T(256)}, u32[]{:S(2)}) copy-start(f32[256]{0:T(256)} %copy-done.16) | copy-start | bytes 3076
  26.6 5.6 %copy-start.19 = (f32[256]{0:T(256)S(1)}, f32[256]{0:T(256)}, u32[]{:S(2)}) copy-start(f32[256]{0:T(256)} %copy-done.18) | copy-start | bytes 3076
  65.5 19.2 %collective-permute-start.22 = (bf16[144,576]{1,0:T(8,128)(2,1)S(1)}, bf16[144,576]{1,0:T(8,128)(2,1)S(1)}, u32[]{:S(2)}, u32[]{:S(2)}) collective-permute-start(bf16[144,576]{1,0:T(8,128)(2,1)S(1)} %slice_select_fusion.4), channel_id=1, source_target_pairs={{0,4},{4,8},{8,12},{12,0},{1,5},{5,9},{9,13},{13,1},{2,6},{6,10},{... | collective-permute-start | bytes 497672 | tf_op jit(solution)/shard_map/ppermute | solution.py:147
  66.7 18.0 %collective-permute-start.23 = (bf16[144,576]{1,0:T(8,128)(2,1)S(1)}, bf16[144,576]{1,0:T(8,128)(2,1)S(1)}, u32[]{:S(2)}, u32[]{:S(2)}) collective-permute-start(bf16[144,576]{1,0:T(8,128)(2,1)S(1)} %slice_select_fusion.4), channel_id=1, source_target_pairs={{0,12},{4,0},{8,4},{12,8},{1,13},{5,1},{9,5},{13,9},{2,14},{6,2},{... | collective-permute-start | bytes 497672 | tf_op jit(solution)/shard_map/ppermute | solution.py:147
  70.4 18.3 %collective-permute-start.4 = (bf16[144,1152]{1,0:T(8,128)(2,1)S(1)}, bf16[144,1152]{1,0:T(8,128)(2,1)S(1)}, u32[]{:S(2)}, u32[]{:S(2)}) collective-permute-start(bf16[144,1152]{1,0:T(8,128)(2,1)S(1)} %slice.238), channel_id=1, source_target_pairs={{0,12},{4,0},{8,4},{12,8},{1,13},{5,1},{9,5},{13,9},{2,14},{6,2},{... | collective-permute-start | bytes 995336 | tf_op jit(solution)/shard_map/ppermute | solution.py:147
  71.9 21.1 %collective-permute-start.3 = (bf16[144,1152]{1,0:T(8,128)(2,1)S(1)}, bf16[144,1152]{1,0:T(8,128)(2,1)S(1)}, u32[]{:S(2)}, u32[]{:S(2)}) collective-permute-start(bf16[144,1152]{1,0:T(8,128)(2,1)S(1)} %slice.237), channel_id=1, source_target_pairs={{0,4},{4,8},{8,12},{12,0},{1,5},{5,9},{9,13},{13,1},{2,6},{6,10},{... | collective-permute-start | bytes 995336 | tf_op jit(solution)/shard_map/ppermute | solution.py:147
  74.5 2.6 %copy-start.4 = (bf16[288,1152]{1,0:T(8,128)(2,1)S(1)}, bf16[288,1152]{1,0:T(8,128)(2,1)}, u32[]{:S(2)}) copy-start(bf16[288,1152]{1,0:T(8,128)(2,1)} %select_bitcast_fusion) | copy-start | bytes 1990660
  74.5 36.8 %collective-permute-start.14 = (bf16[144,1152]{1,0:T(8,128)(2,1)S(1)}, bf16[144,1152]{1,0:T(8,128)(2,1)S(1)}, u32[]{:S(2)}, u32[]{:S(2)}) collective-permute-start(bf16[144,1152]{1,0:T(8,128)(2,1)S(1)} %slice.246), channel_id=1, source_target_pairs={{0,12},{4,0},{8,4},{12,8},{1,13},{5,1},{9,5},{13,9},{2,14},{6,2},{... | collective-permute-start | bytes 995336 | tf_op jit(solution)/shard_map/ppermute | solution.py:147
  84.7 26.7 %collective-permute-start.13 = (bf16[144,1152]{1,0:T(8,128)(2,1)S(1)}, bf16[144,1152]{1,0:T(8,128)(2,1)S(1)}, u32[]{:S(2)}, u32[]{:S(2)}) collective-permute-start(bf16[144,1152]{1,0:T(8,128)(2,1)S(1)} %slice.245), channel_id=1, source_target_pairs={{0,4},{4,8},{8,12},{12,0},{1,5},{5,9},{9,13},{13,1},{2,6},{6,10},{... | collective-permute-start | bytes 995336 | tf_op jit(solution)/shard_map/ppermute | solution.py:147
  84.8 23.5 %collective-permute-start.25 = (bf16[72,576]{1,0:T(8,128)(2,1)S(1)}, bf16[72,576]{1,0:T(8,128)(2,1)S(1)}, u32[]{:S(2)}, u32[]{:S(2)}) collective-permute-start(bf16[72,576]{1,0:T(8,128)(2,1)S(1)} %slice.256), channel_id=1, source_target_pairs={{0,12},{4,0},{8,4},{12,8},{1,13},{5,1},{9,5},{13,9},{2,14},{6,2},{... | collective-permute-start | bytes 248840 | tf_op jit(solution)/shard_map/ppermute | solution.py:147
  88.7 21.1 %collective-permute-start.24 = (bf16[72,576]{1,0:T(8,128)(2,1)S(1)}, bf16[72,576]{1,0:T(8,128)(2,1)S(1)}, u32[]{:S(2)}, u32[]{:S(2)}) collective-permute-start(bf16[72,576]{1,0:T(8,128)(2,1)S(1)} %slice.255), channel_id=1, source_target_pairs={{0,4},{4,8},{8,12},{12,0},{1,5},{5,9},{9,13},{13,1},{2,6},{6,10},{... | collective-permute-start | bytes 248840 | tf_op jit(solution)/shard_map/ppermute | solution.py:147
  98.6 19.3 %copy-start.14 = (f32[1152]{0:T(1024)S(1)}, f32[1152]{0:T(1024)}, u32[]{:S(2)}) copy-start(f32[1152]{0:T(1024)} %get-tuple-element.14) | copy-start | bytes 13828
  98.7 17.5 %collective-permute-start.7 = (bf16[128,1152]{1,0:T(8,128)(2,1)S(1)}, bf16[128,1152]{1,0:T(8,128)(2,1)S(1)}, u32[]{:S(2)}, u32[]{:S(2)}) collective-permute-start(bf16[128,1152]{1,0:T(8,128)(2,1)S(1)} %get-tuple-element.25), channel_id=1, source_target_pairs={{0,18},{2,16},{16,2},{18,0},{1,19},{3,17},{17,3},{19,1},{4,22},{6,... | collective-permute-start | bytes 884744 | tf_op jit(solution)/shard_map/ppermute | solution.py:141
  108.3 8.4 %collective-permute-start.6 = (bf16[128,1152]{1,0:T(8,128)(2,1)S(1)}, bf16[128,1152]{1,0:T(8,128)(2,1)S(1)}, u32[]{:S(2)}, u32[]{:S(2)}) collective-permute-start(bf16[128,1152]{1,0:T(8,128)(2,1)S(1)} %get-tuple-element.26), channel_id=1, source_target_pairs={{0,16},{2,18},{16,0},{18,2},{1,17},{3,19},{17,1},{19,3},{4,20},{6,... | collective-permute-start | bytes 884744 | tf_op jit(solution)/shard_map/ppermute | solution.py:141
  109.8 8.1 %collective-permute-start.5 = (bf16[128,1152]{1,0:T(8,128)(2,1)S(1)}, bf16[128,1152]{1,0:T(8,128)(2,1)S(1)}, u32[]{:S(2)}, u32[]{:S(2)}) collective-permute-start(bf16[128,1152]{1,0:T(8,128)(2,1)S(1)} %get-tuple-element.24), channel_id=1, source_target_pairs={{0,2},{2,0},{16,18},{18,16},{1,3},{3,1},{17,19},{19,17},{4,6},{6,4... | collective-permute-start | bytes 884744 | tf_op jit(solution)/shard_map/ppermute | solution.py:141
  111.3 19.6 %collective-permute-start.15 = (bf16[288,1152]{1,0:T(8,128)(2,1)S(1)}, bf16[288,1152]{1,0:T(8,128)(2,1)S(1)}, u32[]{:S(2)}, u32[]{:S(2)}) collective-permute-start(bf16[288,1152]{1,0:T(8,128)(2,1)S(1)} %copy-done.4), channel_id=1, source_target_pairs={{0,4},{4,8},{8,12},{12,0},{1,5},{5,9},{9,13},{13,1},{2,6},{6,10},{... | collective-permute-start | bytes 1990664 | tf_op jit(solution)/shard_map/ppermute | solution.py:147
  111.4 29.5 %collective-permute-start.16 = (bf16[288,1152]{1,0:T(8,128)(2,1)S(1)}, bf16[288,1152]{1,0:T(8,128)(2,1)S(1)}, u32[]{:S(2)}, u32[]{:S(2)}) collective-permute-start(bf16[288,1152]{1,0:T(8,128)(2,1)S(1)} %copy-done.4), channel_id=1, source_target_pairs={{0,12},{4,0},{8,4},{12,8},{1,13},{5,1},{9,5},{13,9},{2,14},{6,2},{... | collective-permute-start | bytes 1990664 | tf_op jit(solution)/shard_map/ppermute | solution.py:147
  116.1 26.8 %collective-permute-start.26 = (bf16[576,576]{1,0:T(8,128)(2,1)S(1)}, bf16[576,576]{1,0:T(8,128)(2,1)S(1)}, u32[]{:S(2)}, u32[]{:S(2)}) collective-permute-start(bf16[576,576]{1,0:T(8,128)(2,1)S(1)} %bitcast.181), channel_id=1, source_target_pairs={{0,2},{2,0},{1,3},{3,1},{4,6},{6,4},{5,7},{7,5},{8,10},{10,8},{9,1... | collective-permute-start | bytes 1990664 | tf_op jit(solution)/shard_map/ppermute | solution.py:147
  117.9 0.7 copy-start.12
  117.9 0.7 copy-start.13
  118.2 22.7 %copy-start.6 = (bf16[144,1152]{1,0:T(8,128)(2,1)S(1)}, bf16[144,1152]{1,0:T(8,128)(2,1)}, u32[]{:S(2)}) copy-start(bf16[144,1152]{1,0:T(8,128)(2,1)} %slice_select_fusion.3) | copy-start | bytes 995332
  118.8 27.3 %collective-permute-start.10 = (bf16[128,1152]{1,0:T(8,128)(2,1)S(1)}, bf16[128,1152]{1,0:T(8,128)(2,1)S(1)}, u32[]{:S(2)}, u32[]{:S(2)}) collective-permute-start(bf16[128,1152]{1,0:T(8,128)(2,1)S(1)} %add_convert_fusion.1), channel_id=1, source_target_pairs={{0,18},{2,16},{16,2},{18,0},{1,19},{3,17},{17,3},{19,1},{4,22},{6,... | collective-permute-start | bytes 884744 | tf_op jit(solution)/shard_map/ppermute | solution.py:141
  122.3 24.3 %collective-permute-start.9 = (bf16[128,1152]{1,0:T(8,128)(2,1)S(1)}, bf16[128,1152]{1,0:T(8,128)(2,1)S(1)}, u32[]{:S(2)}, u32[]{:S(2)}) collective-permute-start(bf16[128,1152]{1,0:T(8,128)(2,1)S(1)} %add_convert_fusion.1), channel_id=1, source_target_pairs={{0,16},{2,18},{16,0},{18,2},{1,17},{3,19},{17,1},{19,3},{4,20},{6,... | collective-permute-start | bytes 884744 | tf_op jit(solution)/shard_map/ppermute | solution.py:141
  131.0 17.2 %collective-permute-start.8 = (bf16[128,1152]{1,0:T(8,128)(2,1)S(1)}, bf16[128,1152]{1,0:T(8,128)(2,1)S(1)}, u32[]{:S(2)}, u32[]{:S(2)}) collective-permute-start(bf16[128,1152]{1,0:T(8,128)(2,1)S(1)} %add_convert_fusion.1), channel_id=1, source_target_pairs={{0,2},{2,0},{16,18},{18,16},{1,3},{3,1},{17,19},{19,17},{4,6},{6,4... | collective-permute-start | bytes 884744 | tf_op jit(solution)/shard_map/ppermute | solution.py:141
  140.9 37.1 %collective-permute-start.31 = (bf16[144,1152]{1,0:T(8,128)(2,1)S(1)}, bf16[144,1152]{1,0:T(8,128)(2,1)S(1)}, u32[]{:S(2)}, u32[]{:S(2)}) collective-permute-start(bf16[144,1152]{1,0:T(8,128)(2,1)S(1)} %copy-done.6), channel_id=1, source_target_pairs={{0,4},{4,8},{8,12},{12,0},{1,5},{5,9},{9,13},{13,1},{2,6},{6,10},{... | collective-permute-start | bytes 995336 | tf_op jit(solution)/shard_map/ppermute | solution.py:147
  142.9 33.6 %collective-permute-start.32 = (bf16[144,1152]{1,0:T(8,128)(2,1)S(1)}, bf16[144,1152]{1,0:T(8,128)(2,1)S(1)}, u32[]{:S(2)}, u32[]{:S(2)}) collective-permute-start(bf16[144,1152]{1,0:T(8,128)(2,1)S(1)} %copy-done.6), channel_id=1, source_target_pairs={{0,12},{4,0},{8,4},{12,8},{1,13},{5,1},{9,5},{13,9},{2,14},{6,2},{... | collective-permute-start | bytes 995336 | tf_op jit(solution)/shard_map/ppermute | solution.py:147
  146.1 21.4 %collective-permute-start.18 = (bf16[144,1152]{1,0:T(8,128)(2,1)S(1)}, bf16[144,1152]{1,0:T(8,128)(2,1)S(1)}, u32[]{:S(2)}, u32[]{:S(2)}) collective-permute-start(bf16[144,1152]{1,0:T(8,128)(2,1)S(1)} %slice.248), channel_id=1, source_target_pairs={{0,12},{4,0},{8,4},{12,8},{1,13},{5,1},{9,5},{13,9},{2,14},{6,2},{... | collective-permute-start | bytes 995336 | tf_op jit(solution)/shard_map/ppermute | solution.py:147
  146.5 25.8 %collective-permute-start.17 = (bf16[144,1152]{1,0:T(8,128)(2,1)S(1)}, bf16[144,1152]{1,0:T(8,128)(2,1)S(1)}, u32[]{:S(2)}, u32[]{:S(2)}) collective-permute-start(bf16[144,1152]{1,0:T(8,128)(2,1)S(1)} %slice.247), channel_id=1, source_target_pairs={{0,4},{4,8},{8,12},{12,0},{1,5},{5,9},{9,13},{13,1},{2,6},{6,10},{... | collective-permute-start | bytes 995336 | tf_op jit(solution)/shard_map/ppermute | solution.py:147
  148.2 46.7 %collective-permute-start.27 = (bf16[4,1,144,1152]{3,2,1,0:T(8,128)(2,1)S(1)}, bf16[4,1,144,1152]{3,2,1,0:T(8,128)(2,1)S(1)}, u32[]{:S(2)}, u32[]{:S(2)}) collective-permute-start(bf16[4,1,144,1152]{3,2,1,0:T(8,128)(2,1)S(1)} %maximum_select_fusion.2), channel_id=1, source_target_pairs={{0,1},{1,0},{2,3},{3,2},{4,5},{5,4},{6,7},{7,6},{8,9},{9,8},{10,11... | collective-permute-start | bytes 3981320 | tf_op jit(solution)/shard_map/ppermute | solution.py:147
  174.4 16.2 %collective-permute-start.21 = (bf16[128,1152]{1,0:T(8,128)(2,1)S(1)}, bf16[128,1152]{1,0:T(8,128)(2,1)S(1)}, u32[]{:S(2)}, u32[]{:S(2)}) collective-permute-start(bf16[128,1152]{1,0:T(8,128)(2,1)S(1)} %get-tuple-element.22), channel_id=1, source_target_pairs={{0,18},{2,16},{16,2},{18,0},{1,19},{3,17},{17,3},{19,1},{4,22},{6,... | collective-permute-start | bytes 884744 | tf_op jit(solution)/shard_map/ppermute | solution.py:141
  175.9 14.7 %collective-permute-start.20 = (bf16[128,1152]{1,0:T(8,128)(2,1)S(1)}, bf16[128,1152]{1,0:T(8,128)(2,1)S(1)}, u32[]{:S(2)}, u32[]{:S(2)}) collective-permute-start(bf16[128,1152]{1,0:T(8,128)(2,1)S(1)} %get-tuple-element.23), channel_id=1, source_target_pairs={{0,16},{2,18},{16,0},{18,2},{1,17},{3,19},{17,1},{19,3},{4,20},{6,... | collective-permute-start | bytes 884744 | tf_op jit(solution)/shard_map/ppermute | solution.py:141
  176.5 14.2 %copy-start.11 = (f32[1152]{0:T(1024)S(1)}, f32[1152]{0:T(1024)}, u32[]{:S(2)}) copy-start(f32[1152]{0:T(1024)} %get-tuple-element.11) | copy-start | bytes 13828
  176.5 14.2 %collective-permute-start.19 = (bf16[128,1152]{1,0:T(8,128)(2,1)S(1)}, bf16[128,1152]{1,0:T(8,128)(2,1)S(1)}, u32[]{:S(2)}, u32[]{:S(2)}) collective-permute-start(bf16[128,1152]{1,0:T(8,128)(2,1)S(1)} %get-tuple-element.21), channel_id=1, source_target_pairs={{0,2},{2,0},{16,18},{18,16},{1,3},{3,1},{17,19},{19,17},{4,6},{6,4... | collective-permute-start | bytes 884744 | tf_op jit(solution)/shard_map/ppermute | solution.py:141
  178.0 5.4 %collective-permute-start.34 = (bf16[72,1152]{1,0:T(8,128)(2,1)S(1)}, bf16[72,1152]{1,0:T(8,128)(2,1)S(1)}, u32[]{:S(2)}, u32[]{:S(2)}) collective-permute-start(bf16[72,1152]{1,0:T(8,128)(2,1)S(1)} %slice.265), channel_id=1, source_target_pairs={{0,12},{4,0},{8,4},{12,8},{1,13},{5,1},{9,5},{13,9},{2,14},{6,2},{... | collective-permute-start | bytes 497672 | tf_op jit(solution)/shard_map/ppermute | solution.py:147
  183.4 7.1 %collective-permute-start.33 = (bf16[72,1152]{1,0:T(8,128)(2,1)S(1)}, bf16[72,1152]{1,0:T(8,128)(2,1)S(1)}, u32[]{:S(2)}, u32[]{:S(2)}) collective-permute-start(bf16[72,1152]{1,0:T(8,128)(2,1)S(1)} %slice.264), channel_id=1, source_target_pairs={{0,4},{4,8},{8,12},{12,0},{1,5},{5,9},{9,13},{13,1},{2,6},{6,10},{... | collective-permute-start | bytes 497672 | tf_op jit(solution)/shard_map/ppermute | solution.py:147
  190.5 19.6 %collective-permute-start.35 = (bf16[4,1,144,1152]{3,2,1,0:T(8,128)(2,1)S(1)}, bf16[4,1,144,1152]{3,2,1,0:T(8,128)(2,1)S(1)}, u32[]{:S(2)}, u32[]{:S(2)}) collective-permute-start(bf16[4,1,144,1152]{3,2,1,0:T(8,128)(2,1)S(1)} %fusion.38), channel_id=1, source_target_pairs={{0,1},{1,0},{2,3},{3,2},{4,5},{5,4},{6,7},{7,6},{8,9},{9,8},{10,11... | collective-permute-start | bytes 3981320 | tf_op jit(solution)/shard_map/ppermute | solution.py:147
  195.4 4.6 %copy-start.2 = (f32[3,1152]{1,0:T(4,128)S(1)}, f32[3,1152]{1,0:T(4,128)}, u32[]{:S(2)}) copy-start(f32[3,1152]{1,0:T(4,128)} %mod_ref.1) | copy-start | bytes 41476
  196.7 10.0 %all-to-all-start.1 = ((bf16[4,16,1152]{2,1,0:T(8,128)(2,1)}), bf16[4,16,1152]{2,1,0:T(8,128)(2,1)S(1)}, u32[]{:S(2)}, u32[]{:S(2)}) async-start(bf16[4,16,1152]{2,1,0:T(8,128)(2,1)} %bitcast.50), calls=%async_computation.1 | async-start | bytes 294912 | tf_op jit(solution)/shard_map/all_to_all | solution.py:237
  206.7 6.7 %collective-permute-start.30 = (bf16[4,16,1152]{2,1,0:T(8,128)(2,1)S(1)}, bf16[4,16,1152]{2,1,0:T(8,128)(2,1)S(1)}, u32[]{:S(2)}, u32[]{:S(2)}) collective-permute-start(bf16[4,16,1152]{2,1,0:T(8,128)(2,1)S(1)} %all-to-all-done.1), channel_id=1, source_target_pairs={{0,18},{2,16},{16,2},{18,0},{1,19},{3,17},{17,3},{19,1},{4,22},{6,... | collective-permute-start | bytes 442376 | tf_op jit(solution)/shard_map/ppermute | solution.py:141
  208.1 6.7 %collective-permute-start.29 = (bf16[4,16,1152]{2,1,0:T(8,128)(2,1)S(1)}, bf16[4,16,1152]{2,1,0:T(8,128)(2,1)S(1)}, u32[]{:S(2)}, u32[]{:S(2)}) collective-permute-start(bf16[4,16,1152]{2,1,0:T(8,128)(2,1)S(1)} %all-to-all-done.1), channel_id=1, source_target_pairs={{0,16},{2,18},{16,0},{18,2},{1,17},{3,19},{17,1},{19,3},{4,20},{6,... | collective-permute-start | bytes 442376 | tf_op jit(solution)/shard_map/ppermute | solution.py:141
  208.7 6.3 %collective-permute-start.28 = (bf16[4,16,1152]{2,1,0:T(8,128)(2,1)S(1)}, bf16[4,16,1152]{2,1,0:T(8,128)(2,1)S(1)}, u32[]{:S(2)}, u32[]{:S(2)}) collective-permute-start(bf16[4,16,1152]{2,1,0:T(8,128)(2,1)S(1)} %all-to-all-done.1), channel_id=1, source_target_pairs={{0,2},{2,0},{16,18},{18,16},{1,3},{3,1},{17,19},{19,17},{4,6},{6,4... | collective-permute-start | bytes 442376 | tf_op jit(solution)/shard_map/ppermute | solution.py:141
  221.7 7.8 %collective-permute-start.38 = (bf16[4,32,576]{2,1,0:T(8,128)(2,1)S(1)}, bf16[4,32,576]{2,1,0:T(8,128)(2,1)S(1)}, u32[]{:S(2)}, u32[]{:S(2)}) collective-permute-start(bf16[4,32,576]{2,1,0:T(8,128)(2,1)S(1)} %bitcast.195), channel_id=1, source_target_pairs={{0,18},{2,16},{16,2},{18,0},{1,19},{3,17},{17,3},{19,1},{4,22},{6,... | collective-permute-start | bytes 442376 | tf_op jit(solution)/shard_map/ppermute | solution.py:141
  223.2 7.8 %collective-permute-start.37 = (bf16[4,32,576]{2,1,0:T(8,128)(2,1)S(1)}, bf16[4,32,576]{2,1,0:T(8,128)(2,1)S(1)}, u32[]{:S(2)}, u32[]{:S(2)}) collective-permute-start(bf16[4,32,576]{2,1,0:T(8,128)(2,1)S(1)} %bitcast.196), channel_id=1, source_target_pairs={{0,16},{2,18},{16,0},{18,2},{1,17},{3,19},{17,1},{19,3},{4,20},{6,... | collective-permute-start | bytes 442376 | tf_op jit(solution)/shard_map/ppermute | solution.py:141
  224.2 6.8 %collective-permute-start.36 = (bf16[4,32,576]{2,1,0:T(8,128)(2,1)S(1)}, bf16[4,32,576]{2,1,0:T(8,128)(2,1)S(1)}, u32[]{:S(2)}, u32[]{:S(2)}) collective-permute-start(bf16[4,32,576]{2,1,0:T(8,128)(2,1)S(1)} %bitcast.197), channel_id=1, source_target_pairs={{0,2},{2,0},{16,18},{18,16},{1,3},{3,1},{17,19},{19,17},{4,6},{6,4... | collective-permute-start | bytes 442376 | tf_op jit(solution)/shard_map/ppermute | solution.py:141
  226.1 5.8 %copy-start.1 = (f32[13,1152]{1,0:T(8,128)S(1)}, f32[13,1152]{1,0:T(8,128)}, u32[]{:S(2)}) copy-start(f32[13,1152]{1,0:T(8,128)} %param.18) | copy-start | bytes 179716
